TPU v7x, 256 devices: a whole 4x4x8 slice. The times are simulated.
256 devices in a mesh: strip: 64 (over y, x, z_lo, core), lag: 4 (over z_hi).
Axes of the slice: x: 4, y: 4, z: 8 (z_hi: 4, z_lo: 2; z = z_hi * 2 + z_lo), core: 2. Of those that a mesh axis runs over, the one named last changes fastest.
Arguments:
- image_grad: float32 [128, 4096, 1024], P('lag', 'strip'), may hold values from -0.4 to 0.4
- source_field: float32 [2, 4096, 1024], P(None, None, 'strip'), may hold values from -6 to 6
- receiver_field: float32 [2, 4096, 1024], P(None, None, 'strip'), may hold values from -6 to 6
Outputs:
- source_adjoint: float32 [2, 4096, 1024], P(None, 'strip', 'lag')
- receiver_adjoint: float32 [2, 4096, 1024], P(None, 'strip', 'lag')
All inputs are finite; a program needn't handle non-finite values.
Results may differ from a plain program's by a relative error of at most 0.0003.
Values sent between devices are 32-bit elements; how exact they have to be, the bound alone decides.
A program may use at most 128 MiB of HBM per device.

v0:
```python
import jax
import jax.numpy as jnp
from jax import lax
from jax.sharding import PartitionSpec as P

NH = 128


def in_one_piece(arrays, axis, split_dim, concat_dim, along):
    both = jnp.concatenate(arrays, axis=along)
    result, at, gathered = (
        lax.all_to_all(both, axis, split_axis=split_dim, concat_axis=concat_dim, tiled=True),
        0,
        [],
    )
    for a in arrays:
        gathered.append(lax.slice_in_dim(result, at, at + a.shape[along], axis=along))
        at += a.shape[along]
    return tuple(gathered)


def with_halo(cells, sides, width):
    for axis, dim in sides:
        count = lax.axis_size(axis)
        ends = count - 1
        head = lax.slice_in_dim(cells, 0, width, axis=dim)
        tail = lax.slice_in_dim(cells, cells.shape[dim] - width, cells.shape[dim], axis=dim)
        cells = jnp.concatenate(
            [
                lax.ppermute(tail, axis, [(i, (i + 1) % count) for i in range(ends)]),
                cells,
                lax.ppermute(head, axis, [((i + 1) % count, i) for i in range(ends)]),
            ],
            axis=dim,
        )
    return cells


def cut_along(value, dim, size):
    before, after = (value.shape[:dim], value.shape[dim + 1 :])
    return jnp.moveaxis(value.reshape(*before, size, -1, *after), dim, 0)


def summed_on_arrival(value, axis, dim):
    size = lax.axis_size(axis)
    blocks = lax.all_to_all(cut_along(value, dim, size), axis, 0, 0, tiled=True)
    return jnp.sum(blocks, axis=0)


def side_by_side(arrays, axis, dim, along):
    ends, at = ([], 0)
    for a in arrays[:-1]:
        at += a.shape[along]
        ends.append(at)
    both = jnp.concatenate(arrays, axis=along)
    return tuple(jnp.split(summed_on_arrival(both, axis, dim), ends, axis=along))


def pad_cells(values, margin):
    return jnp.pad(values, [(0, 0)] * (values.ndim - 1) + [(margin, margin)])


def shift_cells(padded_values, offset, margin, width_cells):
    start = margin + offset
    return lax.dynamic_slice_in_dim(padded_values, start, width_cells, padded_values.ndim - 1)


def local(image_grad, source_field, receiver_field):
    lag_count = image_grad.shape[0]
    depth_rows = image_grad.shape[1]
    width_cells = image_grad.shape[2]
    margin = NH
    source_t, receiver_t = in_one_piece((source_field, receiver_field), "strip", 1, 2, 0)
    source = pad_cells(source_t, margin)
    receiver = pad_cells(receiver_t, margin)
    padded = with_halo(image_grad, (("strip", 1),), 1)
    center = padded[:, 1:-1]
    sideways = jnp.pad(center, ((0, 0), (0, 0), (1, 1)))
    filtered = 2.0 * center - 0.25 * (
        padded[:, 2:] + padded[:, :-2] + sideways[:, :, 2:] + sideways[:, :, :-2]
    )
    filter_pad = pad_cells(filtered, margin)
    first_lag = lax.axis_index("lag") * lag_count - NH // 2
    empty_sum = jnp.zeros((source.shape[0], depth_rows, width_cells), jnp.float32)

    def group_step(group_at, totals):
        source_total, receiver_total = totals
        for within in range(4):
            position = group_at * 4 + within
            slab_now = lax.dynamic_index_in_dim(filter_pad, position, 0, keepdims=False)
            offset = first_lag + position
            source_total = source_total + shift_cells(slab_now, offset, margin, width_cells)[
                None
            ] * shift_cells(receiver, 2 * offset, margin, width_cells)
            receiver_total = receiver_total + shift_cells(slab_now, -offset, margin, width_cells)[
                None
            ] * shift_cells(source, -2 * offset, margin, width_cells)
        return (source_total, receiver_total)

    totals = lax.fori_loop(0, lag_count // 4, group_step, (empty_sum, empty_sum))
    source_adjoint, receiver_adjoint = side_by_side((totals[0], totals[1]), "lag", 2, 0)
    return (source_adjoint, receiver_adjoint)


def solution(mesh):
    in_specs = (P("lag", "strip", None), P(None, None, "strip"), P(None, None, "strip"))
    out_specs = (P(None, "strip", "lag"), P(None, "strip", "lag"))
    return jax.shard_map(local, mesh=mesh, in_specs=in_specs, out_specs=out_specs, check_vma=False)
```

profile of v0, /device:TPU:2, one launch (start us, length us, event | category | flops | bytes accessed | tf_op | source)
XLA Modules:
  0.0 186.8 jit_solution(15975732312872675093)
XLA Ops:
  1.9 5.9 %copy.20 = f32[4,4096,16]{2,0,1:T(4,128)} copy(f32[4,4096,16]{1,2,0:T(8,128)S(1)} %pad_maximum_fusion.2) | data formatting | bytes 2097152 | tf_op jit(solution)/shard_map/concatenate | solution.py:10
  7.8 8.9 %reshape.26 = f32[64,1,4096]{2,1,0:T(1,128)} reshape(f32[4096,4,16]{2,1,0:T(4,128)} %bitcast.26) | data formatting | bytes 2097152
  16.7 9.4 %all-to-all-start = ((f32[64,1,4096]{2,1,0:T(1,128)}), f32[64,1,4096]{2,1,0:T(1,128)S(1)}, u32[]{:S(2)}, u32[]{:S(2)}) async-start(f32[64,1,4096]{2,1,0:T(1,128)} %reshape.26), calls=%async_computation | async-start | bytes 2097152 | tf_op jit(solution)/shard_map/all_to_all | solution.py:12
  27.9 3.1 %collective-permute-start = (f32[32,1,1024]{2,1,0:T(1,128)S(1)}, f32[32,1,1024]{2,1,0:T(1,128)S(1)}, u32[]{:S(2)}, u32[]{:S(2)}) collective-permute-start(f32[32,1,1024]{2,1,0:T(1,128)S(1)} %get-tuple-element.318), channel_id=1, source_target_pairs={{4,0},{8,4},{12,8},{16,12},{20,16},{24,20},{28,24},{32,28},{36,32}... | collective-permute-start | bytes 393224 | tf_op jit(solution)/shard_map/ppermute | solution.py:32
  33.1 7.4 %collective-permute-done = f32[32,1,1024]{2,1,0:T(1,128)S(1)} collective-permute-done((f32[32,1,1024]{2,1,0:T(1,128)S(1)}, f32[32,1,1024]{2,1,0:T(1,128)S(1)}, u32[]{:S(2)}, u32[]{:S(2)}) %collective-permute-start) | collective-permute-done | bytes 131104 | tf_op jit(solution)/shard_map/ppermute | solution.py:32
  41.8 20.9 %fusion.9 = f32[32,64,1024]{2,1,0:T(8,128)} fusion(f32[32,64,1024]{2,1,0:T(8,128)} %param.5, f32[32,1,1024]{2,1,0:T(1,128)S(1)} %collective-permute-done.1, f32[32,1,1024]{2,1,0:T(1,128)S(1)} %collective-permute-done), kind=kLoop, calls=%fused_computation.21 | loop fusion | flops 16777216 | bytes 17039360 | tf_op jit(solution)/shard_map/sub | solution.py:79
  62.7 8.7 %pad.16 = f32[32,64,1280]{2,1,0:T(8,128)} pad(f32[32,64,1024]{2,1,0:T(8,128)} %fusion.9, f32[]{:T(128)} %constant.562.clone.1), padding=0_0x0_0x128_128 | pad | bytes 18874372 | tf_op jit(solution)/shard_map/jit(_pad)/pad | solution.py:60
  71.9 3.2 %reduce = f32[64,4096]{1,0:T(8,128)S(1)} reduce(f32[64,1,4096]{2,1,0:T(1,128)S(1)} %all-to-all-done, f32[]{:T(128)} %broadcast.20), dimensions={1}, to_apply=%all_to_all.14.reduce_sub_computation | reduce | bytes 2097156 | tf_op jit(solution)/shard_map/all_to_all | solution.py:12
  75.2 7.2 %reshape.27 = f32[4096,4,16]{2,1,0:T(4,128)} reshape(f32[64,4096]{1,0:T(8,128)S(1)} %reduce) | data formatting | bytes 2097152
  82.4 6.8 %copy.21 = f32[4,64,64,16]{2,3,1,0:T(8,128)S(1)} copy(f32[4,64,64,16]{3,0,2,1:T(4,128)} %bitcast.25) | data formatting | bytes 2097152 | tf_op jit(solution)/shard_map/all_to_all | solution.py:12
  92.3 55.7 %while.19 = (s32[]{:T(128)}, f32[2,64,1024]{2,1,0:T(8,128)}, f32[2,64,1024]{2,1,0:T(8,128)}, s32[]{:T(128)}, f32[32,64,1280]{2,1,0:T(8,128)}, /*index=5*/f32[2,6...) while((s32[]{:T(128)}, f32[2,64,1024]{2,1,0:T(8,128)}, ...), condition=%wide.region_1.2_spmd.clone, body=%wide.region_0.1_spmd.clone.sunk | while | flops 2359407 | bytes 12584480 | solution.py:100
  99.8 2.5 %fusion.17 = f32[2,64,1024]{2,1,0:T(8,128)} fusion(f32[2,64,1024]{2,1,0:T(8,128)} %get-tuple-element.406, f32[2,64,1280]{2,1,0:T(8,128)S(1)} %get-tuple-element.431, s32[]{:T(128)S(6)} %select_n.337, s32[]{:T(128)S(6)} %select_n.338, s32[]{:T(128)S(6)} %select_n.339, s32[]{:T(128)S(6)} %select_n.340, f32[64,1024]{1,0:T(8,128)S(1)} %get-tuple-element.379, ...), kind=kLoop, calls=%fused_computation.3.clone.1 | loop fusion | flops 1179648 | bytes 4194321 | tf_op jit(solution)/shard_map/while/body/eval_jaxpr/add | solution.py:95
  102.3 2.4 %fusion.16 = f32[2,64,1024]{2,1,0:T(8,128)} fusion(f32[2,64,1024]{2,1,0:T(8,128)} %get-tuple-element.405, f32[2,64,1280]{2,1,0:T(8,128)S(1)} %get-tuple-element.430, s32[]{:T(128)S(6)} %select_n.309, s32[]{:T(128)S(6)} %select_n.310, s32[]{:T(128)S(6)} %select_n.311, s32[]{:T(128)S(6)} %select_n.312, f32[64,1024]{1,0:T(8,128)S(1)} %get-tuple-element.375, ...), kind=kLoop, calls=%fused_computation.7.clone.1 | loop fusion | flops 1179648 | bytes 4194321 | tf_op jit(solution)/shard_map/while/body/eval_jaxpr/add | solution.py:92
  107.0 2.5 %fusion.17 = f32[2,64,1024]{2,1,0:T(8,128)} fusion(f32[2,64,1024]{2,1,0:T(8,128)} %get-tuple-element.406, f32[2,64,1280]{2,1,0:T(8,128)S(1)} %get-tuple-element.431, s32[]{:T(128)S(6)} %select_n.337, s32[]{:T(128)S(6)} %select_n.338, s32[]{:T(128)S(6)} %select_n.339, s32[]{:T(128)S(6)} %select_n.340, f32[64,1024]{1,0:T(8,128)S(1)} %get-tuple-element.379, ...), kind=kLoop, calls=%fused_computation.3.clone.1 | loop fusion | flops 1179648 | bytes 4194321 | tf_op jit(solution)/shard_map/while/body/eval_jaxpr/add | solution.py:95
  109.5 2.4 %fusion.16 = f32[2,64,1024]{2,1,0:T(8,128)} fusion(f32[2,64,1024]{2,1,0:T(8,128)} %get-tuple-element.405, f32[2,64,1280]{2,1,0:T(8,128)S(1)} %get-tuple-element.430, s32[]{:T(128)S(6)} %select_n.309, s32[]{:T(128)S(6)} %select_n.310, s32[]{:T(128)S(6)} %select_n.311, s32[]{:T(128)S(6)} %select_n.312, f32[64,1024]{1,0:T(8,128)S(1)} %get-tuple-element.375, ...), kind=kLoop, calls=%fused_computation.7.clone.1 | loop fusion | flops 1179648 | bytes 4194321 | tf_op jit(solution)/shard_map/while/body/eval_jaxpr/add | solution.py:92
  114.3 2.5 %fusion.17 = f32[2,64,1024]{2,1,0:T(8,128)} fusion(f32[2,64,1024]{2,1,0:T(8,128)} %get-tuple-element.406, f32[2,64,1280]{2,1,0:T(8,128)S(1)} %get-tuple-element.431, s32[]{:T(128)S(6)} %select_n.337, s32[]{:T(128)S(6)} %select_n.338, s32[]{:T(128)S(6)} %select_n.339, s32[]{:T(128)S(6)} %select_n.340, f32[64,1024]{1,0:T(8,128)S(1)} %get-tuple-element.379, ...), kind=kLoop, calls=%fused_computation.3.clone.1 | loop fusion | flops 1179648 | bytes 4194321 | tf_op jit(solution)/shard_map/while/body/eval_jaxpr/add | solution.py:95
  116.7 2.4 %fusion.16 = f32[2,64,1024]{2,1,0:T(8,128)} fusion(f32[2,64,1024]{2,1,0:T(8,128)} %get-tuple-element.405, f32[2,64,1280]{2,1,0:T(8,128)S(1)} %get-tuple-element.430, s32[]{:T(128)S(6)} %select_n.309, s32[]{:T(128)S(6)} %select_n.310, s32[]{:T(128)S(6)} %select_n.311, s32[]{:T(128)S(6)} %select_n.312, f32[64,1024]{1,0:T(8,128)S(1)} %get-tuple-element.375, ...), kind=kLoop, calls=%fused_computation.7.clone.1 | loop fusion | flops 1179648 | bytes 4194321 | tf_op jit(solution)/shard_map/while/body/eval_jaxpr/add | solution.py:92
  121.5 2.5 %fusion.17 = f32[2,64,1024]{2,1,0:T(8,128)} fusion(f32[2,64,1024]{2,1,0:T(8,128)} %get-tuple-element.406, f32[2,64,1280]{2,1,0:T(8,128)S(1)} %get-tuple-element.431, s32[]{:T(128)S(6)} %select_n.337, s32[]{:T(128)S(6)} %select_n.338, s32[]{:T(128)S(6)} %select_n.339, s32[]{:T(128)S(6)} %select_n.340, f32[64,1024]{1,0:T(8,128)S(1)} %get-tuple-element.379, ...), kind=kLoop, calls=%fused_computation.3.clone.1 | loop fusion | flops 1179648 | bytes 4194321 | tf_op jit(solution)/shard_map/while/body/eval_jaxpr/add | solution.py:95
  124.0 2.4 %fusion.16 = f32[2,64,1024]{2,1,0:T(8,128)} fusion(f32[2,64,1024]{2,1,0:T(8,128)} %get-tuple-element.405, f32[2,64,1280]{2,1,0:T(8,128)S(1)} %get-tuple-element.430, s32[]{:T(128)S(6)} %select_n.309, s32[]{:T(128)S(6)} %select_n.310, s32[]{:T(128)S(6)} %select_n.311, s32[]{:T(128)S(6)} %select_n.312, f32[64,1024]{1,0:T(8,128)S(1)} %get-tuple-element.375, ...), kind=kLoop, calls=%fused_computation.7.clone.1 | loop fusion | flops 1179648 | bytes 4194321 | tf_op jit(solution)/shard_map/while/body/eval_jaxpr/add | solution.py:92
  128.7 2.5 %fusion.17 = f32[2,64,1024]{2,1,0:T(8,128)} fusion(f32[2,64,1024]{2,1,0:T(8,128)} %get-tuple-element.406, f32[2,64,1280]{2,1,0:T(8,128)S(1)} %get-tuple-element.431, s32[]{:T(128)S(6)} %select_n.337, s32[]{:T(128)S(6)} %select_n.338, s32[]{:T(128)S(6)} %select_n.339, s32[]{:T(128)S(6)} %select_n.340, f32[64,1024]{1,0:T(8,128)S(1)} %get-tuple-element.379, ...), kind=kLoop, calls=%fused_computation.3.clone.1 | loop fusion | flops 1179648 | bytes 4194321 | tf_op jit(solution)/shard_map/while/body/eval_jaxpr/add | solution.py:95
  136.0 2.5 %fusion.17 = f32[2,64,1024]{2,1,0:T(8,128)} fusion(f32[2,64,1024]{2,1,0:T(8,128)} %get-tuple-element.406, f32[2,64,1280]{2,1,0:T(8,128)S(1)} %get-tuple-element.431, s32[]{:T(128)S(6)} %select_n.337, s32[]{:T(128)S(6)} %select_n.338, s32[]{:T(128)S(6)} %select_n.339, s32[]{:T(128)S(6)} %select_n.340, f32[64,1024]{1,0:T(8,128)S(1)} %get-tuple-element.379, ...), kind=kLoop, calls=%fused_computation.3.clone.1 | loop fusion | flops 1179648 | bytes 4194321 | tf_op jit(solution)/shard_map/while/body/eval_jaxpr/add | solution.py:95
  143.1 2.5 %fusion.17 = f32[2,64,1024]{2,1,0:T(8,128)} fusion(f32[2,64,1024]{2,1,0:T(8,128)} %get-tuple-element.406, f32[2,64,1280]{2,1,0:T(8,128)S(1)} %get-tuple-element.431, s32[]{:T(128)S(6)} %select_n.337, s32[]{:T(128)S(6)} %select_n.338, s32[]{:T(128)S(6)} %select_n.339, s32[]{:T(128)S(6)} %select_n.340, f32[64,1024]{1,0:T(8,128)S(1)} %get-tuple-element.379, ...), kind=kLoop, calls=%fused_computation.3.clone.1 | loop fusion | flops 1179648 | bytes 4194321 | tf_op jit(solution)/shard_map/while/body/eval_jaxpr/add | solution.py:95
  145.6 2.4 %fusion.16 = f32[2,64,1024]{2,1,0:T(8,128)} fusion(f32[2,64,1024]{2,1,0:T(8,128)} %get-tuple-element.405, f32[2,64,1280]{2,1,0:T(8,128)S(1)} %get-tuple-element.430, s32[]{:T(128)S(6)} %select_n.309, s32[]{:T(128)S(6)} %select_n.310, s32[]{:T(128)S(6)} %select_n.311, s32[]{:T(128)S(6)} %select_n.312, f32[64,1024]{1,0:T(8,128)S(1)} %get-tuple-element.375, ...), kind=kLoop, calls=%fused_computation.7.clone.1 | loop fusion | flops 1179648 | bytes 4194321 | tf_op jit(solution)/shard_map/while/body/eval_jaxpr/add | solution.py:92
  150.1 35.9 %all_to_all.20 = f32[4,4,64,256]{3,2,1,0:T(8,128)S(1)} all-to-all(f32[4,4,64,256]{3,2,1,0:T(8,128)S(1)} %copy.24), channel_id=1, replica_groups=mesh['strip'=64,'lag'=4] {'lag'}, dimensions={0} | all-to-all | bytes 2097152 | tf_op jit(solution)/shard_map/all_to_all | solution.py:46
  (30 shorter events, 38.6 us)
Async XLA Ops:
  16.7 54.7 %all-to-all-start = ((f32[64,1,4096]{2,1,0:T(1,128)}), f32[64,1,4096]{2,1,0:T(1,128)S(1)}, u32[]{:S(2)}, u32[]{:S(2)}) async-start(f32[64,1,4096]{2,1,0:T(1,128)} %reshape.26), calls=%async_computation | async-start | bytes 2097152 | tf_op jit(solution)/shard_map/all_to_all | solution.py:12
  27.9 12.6 %collective-permute-start = (f32[32,1,1024]{2,1,0:T(1,128)S(1)}, f32[32,1,1024]{2,1,0:T(1,128)S(1)}, u32[]{:S(2)}, u32[]{:S(2)}) collective-permute-start(f32[32,1,1024]{2,1,0:T(1,128)S(1)} %get-tuple-element.318), channel_id=1, source_target_pairs={{4,0},{8,4},{12,8},{16,12},{20,16},{24,20},{28,24},{32,28},{36,32}... | collective-permute-start | bytes 393224 | tf_op jit(solution)/shard_map/ppermute | solution.py:32
  31.0 10.9 %collective-permute-start.1 = (f32[32,1,1024]{2,1,0:T(1,128)S(1)}, f32[32,1,1024]{2,1,0:T(1,128)S(1)}, u32[]{:S(2)}, u32[]{:S(2)}) collective-permute-start(f32[32,1,1024]{2,1,0:T(1,128)S(1)} %get-tuple-element.319), channel_id=1, source_target_pairs={{0,4},{4,8},{8,12},{12,16},{16,20},{20,24},{24,28},{28,32},{32,36}... | collective-permute-start | bytes 393224 | tf_op jit(solution)/shard_map/ppermute | solution.py:30
where the time goes:
time: 188 us; the launch traced here: 187 us
  other arithmetic  64 us (34%)
  local copies, waits for them, and re-layouts  62.3 us (33%)
  blocking collectives  35.9 us (19%)
  starting transfers between devices  14.6 us (8%)
  waiting for transfers between devices  8.74 us (5%)
    all_to_all x1, blocking collectives, summed_on_arrival(): blocks = lax.all_to_all(cut_along(value, dim, size), axis, 0, 0, tiled=True)  35.9 us
    sub x1, other arithmetic, local(): 2.0 * center  20.9 us
    add x8, other arithmetic, group_step(): receiver_total + shift_cells(slab_now, -offset, margin, width_cells)[None...  18.7 us
    add x8, other arithmetic, group_step(): source_total + shift_cells(slab_now, offset, margin, width_cells)[None] *...  18.5 us
    mul x8, local copies, waits for them, and re-layouts, group_step(): shift_cells(slab_now, -offset, margin, width_cells)[None]  18 us
    unnamed x4, local copies, waits for them, and re-layouts  18 us
    all_to_all x1, starting transfers between devices, in_one_piece(): lax.all_to_all(both, axis, split_axis=split_dim, concat_axis=concat_dim,...  9.38 us
    pad x3, local copies, waits for them, and re-layouts, pad_cells(): return jnp.pad(values, [(0, 0)] * (values.ndim - 1) + [(margin, margin)])  8.77 us
  transfers between devices with their start and end apart: 3, of which 2 were waited for; matrix products, arithmetic and copies ran while one was open for 17% of the time, Pallas kernels for 0%

commit v1 on v0

v1 whole, which is shorter than its diff:
```python
import functools

import jax
import jax.numpy as jnp
from jax import lax
from jax.experimental import pallas as pl
from jax.experimental.pallas import tpu as pltpu
from jax.sharding import PartitionSpec as P

MESH = pl.DeviceIdType.MESH
F32 = jnp.float32

STRIPS = 64
LAGS = 4
NK = 32
ROWS = 64
NX = 1024
XB = NX // 128
COLS = NX // STRIPS
PADX = 128
PADF = 64
SLOT = 80
OUTX = NX // LAGS
SUB = 64
CHUNKS = 8
KC = NK // CHUNKS


def copy_bytes(ref, sem):
    return pltpu.make_async_copy(ref, ref, sem)


def kernel(
    grad, source, receiver, out_s, out_r,
    edge, tiles, filt, packed, raw, field, halo_out, halo_in,
    part, relay, near_in, own,
    edge_sem, raw_sem, load_sem, a2a_send, a2a_recv,
    halo_send, halo_recv, rs_send, rs_recv,
):
    me = lax.axis_index("strip")
    lag = lax.axis_index("lag")
    up_lag = lax.rem(lag + 1, LAGS)
    down_lag = lax.rem(lag + LAGS - 1, LAGS)
    next_strip = lax.rem(me + 1, STRIPS)
    prev_strip = lax.rem(me + STRIPS - 1, STRIPS)

    barrier = pltpu.get_barrier_semaphore()

    def greet(d, carry):
        pl.semaphore_signal(
            barrier, inc=1, device_id=(lax.rem(me + d, STRIPS), lag), device_id_type=MESH
        )
        return carry

    lax.fori_loop(1, STRIPS, greet, 0)
    for other in (up_lag, down_lag):
        pl.semaphore_signal(barrier, inc=1, device_id=(me, other), device_id_type=MESH)

    for b in range(XB):
        lanes = pl.ds(128 * b, 128)
        pltpu.make_async_copy(grad.at[:, 0:8, lanes], edge.at[0, :, b], edge_sem).start()
        pltpu.make_async_copy(
            grad.at[:, ROWS - 8 : ROWS, lanes], edge.at[1, :, b], edge_sem
        ).start()
    pltpu.make_async_copy(source, raw.at[0], raw_sem).start()
    pltpu.make_async_copy(receiver, raw.at[1], raw_sem).start()
    for c in range(CHUNKS):
        for b in range(XB):
            pltpu.make_async_copy(
                grad.at[c * KC : (c + 1) * KC, :, 128 * b : 128 * (b + 1)],
                tiles.at[c * KC : (c + 1) * KC, b, 8 : 8 + ROWS, :],
                load_sem.at[c],
            ).start()

    for f in range(2):
        field[f, 0:PADX, :] = jnp.zeros((PADX, 128), F32)
        field[f, PADX + NX :, :] = jnp.zeros((PADX, 128), F32)
    filt[0:PADF, :] = jnp.zeros((PADF, 128), F32)
    filt[PADF + NK * NX :, :] = jnp.zeros((PADF, 128), F32)

    copy_bytes(edge, edge_sem).wait()
    flat = edge.reshape(2 * NK * XB * 8, 128)
    halo_out[0] = flat[pl.ds(0, NK * XB, stride=8), :]
    halo_out[1] = flat[pl.ds(NK * XB * 8 + 7, NK * XB, stride=8), :]

    copy_bytes(raw, raw_sem).wait()
    low = lax.broadcasted_iota(jnp.int32, (COLS, 128), 1) < ROWS

    def pack(j, carry):
        lanes = pl.ds(pl.multiple_of(128 * j, 128), 128)
        for f in range(2):
            first = raw[f, 0, :, lanes]
            second = raw[f, 1, :, lanes]
            packed[2 * j, f] = jnp.where(low, first, pltpu.roll(second, ROWS, 1))
            packed[2 * j + 1, f] = jnp.where(low, pltpu.roll(first, ROWS, 1), second)
        return carry

    lax.fori_loop(0, STRIPS // 2, pack, 0)
    here = pl.ds(pl.multiple_of(PADX + COLS * me, 8), COLS)
    for f in range(2):
        field[f, here, :] = packed[me, f]

    pl.semaphore_wait(barrier, STRIPS - 1 + 2)

    halo_up = pltpu.make_async_remote_copy(
        halo_out.at[1], halo_in.at[0], halo_send.at[0], halo_recv.at[0],
        device_id=(next_strip, lag), device_id_type=MESH,
    )
    halo_down = pltpu.make_async_remote_copy(
        halo_out.at[0], halo_in.at[1], halo_send.at[1], halo_recv.at[1],
        device_id=(prev_strip, lag), device_id_type=MESH,
    )
    halo_up.start()
    halo_down.start()

    def send(d, carry):
        to = lax.rem(me + d, STRIPS)
        pltpu.make_async_remote_copy(
            packed.at[to], field.at[:, here, :], a2a_send, a2a_recv,
            device_id=(to, lag), device_id_type=MESH,
        ).start()
        return carry

    lax.fori_loop(1, STRIPS, send, 0)

    halo_up.wait()
    halo_down.wait()
    halo_in[0] = jnp.where(me == 0, 0.0, halo_in[0])
    halo_in[1] = jnp.where(me == STRIPS - 1, 0.0, halo_in[1])

    lane = lax.broadcasted_iota(jnp.int32, (ROWS, 128), 1)
    wide = lax.broadcasted_iota(jnp.int32, (128, 128), 1) < ROWS

    def filtered(k):
        centers = []
        for b in range(XB):
            tiles[k, b, 7:8, :] = halo_in[0, pl.ds(k * XB + b, 1), :]
            tiles[k, b, 8 + ROWS : 9 + ROWS, :] = halo_in[1, pl.ds(k * XB + b, 1), :]
        out = []
        for b in range(XB):
            center = tiles[k, b, 8 : 8 + ROWS, :]
            above = tiles[k, b, 7 : 7 + ROWS, :]
            below = tiles[k, b, 9 : 9 + ROWS, :]
            left = pltpu.roll(center, 1, 1)
            right = pltpu.roll(center, 127, 1)
            before = (
                pltpu.roll(tiles[k, b - 1, 8 : 8 + ROWS, :], 1, 1) if b else jnp.zeros_like(left)
            )
            after = (
                pltpu.roll(tiles[k, b + 1, 8 : 8 + ROWS, :], 127, 1)
                if b < XB - 1
                else jnp.zeros_like(left)
            )
            left = jnp.where(lane == 0, before, left)
            right = jnp.where(lane == 127, after, right)
            out.append(2.0 * center - 0.25 * ((above + below) + (left + right)))
        return out

    def pair(p, carry):
        one = filtered(2 * p)
        two = filtered(2 * p + 1)
        for b in range(XB):
            both = jnp.concatenate([one[b], two[b]], axis=0).T
            turned = pltpu.roll(both, ROWS, 1)
            base = PADF + 2 * p * NX + 128 * b
            filt[pl.ds(pl.multiple_of(base, 8), 128), :] = jnp.where(wide, both, turned)
            filt[pl.ds(pl.multiple_of(base + NX, 8), 128), :] = jnp.where(wide, turned, both)
        return carry

    for c in range(CHUNKS):
        copy_bytes(tiles.at[c * KC : (c + 1) * KC, :, 8 : 8 + ROWS, :], load_sem.at[c]).wait()
        lax.fori_loop(c * KC // 2, (c + 1) * KC // 2, pair, 0)

    copy_bytes(packed.at[0 : STRIPS - 1], a2a_recv).wait()

    first_lag = lag * NK - NK * LAGS // 2

    def products(block, put):
        def sub(i, carry):
            x = block * OUTX + i * SUB

            def step(k, sums):
                h = first_lag + k
                at = PADF + k * NX + x
                s = sums[0] + filt[pl.ds(at + h, SUB), :] * field[1, pl.ds(PADX + x + 2 * h, SUB), :]
                r = sums[1] + filt[pl.ds(at - h, SUB), :] * field[0, pl.ds(PADX + x - 2 * h, SUB), :]
                return s, r

            zero = jnp.zeros((SUB, 128), F32)
            s, r = lax.fori_loop(0, NK, step, (zero, zero), unroll=4)
            put(pl.ds(pl.multiple_of(i * SUB, SUB), SUB), s, r)
            return carry

        lax.fori_loop(0, OUTX // SUB, sub, 0)

    def put_part(n):
        def put(rows, s, r):
            part[n, 0, rows, :] = s
            part[n, 1, rows, :] = r

        return put

    def lag_copy(n, src, dst, to):
        return pltpu.make_async_remote_copy(
            src, dst, rs_send.at[n], rs_recv.at[n], device_id=(me, to), device_id_type=MESH
        )

    products(lax.rem(lag + 2, LAGS), put_part(0))
    far_s = lag_copy(0, part.at[0, 0], relay.at[0], up_lag)
    far_r = lag_copy(1, part.at[0, 1], relay.at[1], down_lag)
    far_s.start()
    far_r.start()
    products(up_lag, put_part(1))
    up_r = lag_copy(2, part.at[1, 1], near_in.at[0, 1], up_lag)
    up_r.start()
    products(down_lag, put_part(2))
    down_s = lag_copy(3, part.at[2, 0], near_in.at[1, 0], down_lag)
    down_s.start()

    far_s.wait_recv()
    part[1, 0] = part[1, 0] + relay[0]
    up_s = lag_copy(4, part.at[1, 0], near_in.at[0, 0], up_lag)
    up_s.start()
    far_r.wait_recv()
    part[2, 1] = part[2, 1] + relay[1]
    down_r = lag_copy(5, part.at[2, 1], near_in.at[1, 1], down_lag)
    down_r.start()

    def put_own(rows, s, r):
        own[0, rows, :] = s
        own[1, rows, :] = r

    products(lag, put_own)

    for f, out, copies in ((0, out_s, (down_s, up_s)), (1, out_r, (up_r, down_r))):
        for copy in copies:
            copy.wait_recv()
        for b in range(OUTX // 128):
            rows = pl.ds(128 * b, 128)
            total = own[f, rows, :] + near_in[0, f, rows, :] + near_in[1, f, rows, :]
            turned = total.T
            out[0, :, rows] = turned[0:ROWS]
            out[1, :, rows] = turned[ROWS:]

    for copy in (far_s, far_r, up_r, down_s, up_s, down_r):
        copy.wait_send()
    copy_bytes(packed.at[0 : STRIPS - 1], a2a_send).wait()


def local(image_grad, source_field, receiver_field):
    vmem = pltpu.VMEM
    dma = pltpu.SemaphoreType.DMA
    out = jax.ShapeDtypeStruct((2, ROWS, OUTX), F32)
    return pl.pallas_call(
        kernel,
        out_shape=(out, out),
        in_specs=[pl.BlockSpec(memory_space=pl.ANY)] * 3,
        out_specs=[pl.BlockSpec(memory_space=pltpu.VMEM)] * 2,
        scratch_shapes=[
            vmem((2, NK, XB, 8, 128), F32),
            vmem((NK, XB, SLOT, 128), F32),
            vmem((NK * NX + 2 * PADF, 128), F32),
            vmem((STRIPS, 2, COLS, 128), F32),
            vmem((2, 2, COLS, STRIPS * ROWS), F32),
            vmem((2, NX + 2 * PADX, 128), F32),
            vmem((2, NK * XB, 128), F32),
            vmem((2, NK * XB, 128), F32),
            vmem((3, 2, OUTX, 128), F32),
            vmem((2, OUTX, 128), F32),
            vmem((2, 2, OUTX, 128), F32),
            vmem((2, OUTX, 128), F32),
            dma,
            dma,
            dma((CHUNKS,)),
            dma,
            dma,
            dma((2,)),
            dma((2,)),
            dma((6,)),
            dma((6,)),
        ],
        compiler_params=pltpu.CompilerParams(
            collective_id=0, has_side_effects=True, vmem_limit_bytes=60 << 20
        ),
        name="adjoint",
    )(image_grad, jnp.swapaxes(source_field, 1, 2), jnp.swapaxes(receiver_field, 1, 2))


def solution(mesh):
    in_specs = (P("lag", "strip", None), P(None, None, "strip"), P(None, None, "strip"))
    out_specs = (P(None, "strip", "lag"), P(None, "strip", "lag"))
    return jax.shard_map(local, mesh=mesh, in_specs=in_specs, out_specs=out_specs, check_vma=False)
```

time: 188 us -> 54.1 us (0.29)
  the two profiles are of different devices: /device:TPU:2 before, /device:TPU:1 now
where the time goes in v1:
time: 54.1 us; the launch traced here: 54 us
  Pallas kernels  50.2 us (93%)
  local copies, waits for them, and re-layouts  3.14 us (6%)
  between operations  0.64 us (1%)
    pallas_call x1, Pallas kernels, local(): pl.pallas_call(kernel, out_shape=(out, out), in_specs=[pl.BlockSpec(memor...  50.2 us
    unnamed x2, local copies, waits for them, and re-layouts  3.14 us

profile of v1, /device:TPU:1, one launch (start us, length us, event | category | flops | bytes accessed | tf_op | source)
XLA Modules:
  0.0 54.0 jit_solution(779817403723834284)
XLA Ops:
  0.6 50.2 %adjoint.1 = (f32[2,64,256]{2,1,0:T(8,128)}, f32[2,64,256]{2,1,0:T(8,128)}) custom-call(f32[32,64,1024]{2,1,0:T(8,128)} %grad.1, f32[2,16,4096]{2,1,0:T(8,128)} %bitcast.2, f32[2,16,4096]{2,1,0:T(8,128)} %bitcast.3), custom_call_target="tpu_custom_call" | custom-call | tf_op jit(solution)/shard_map/adjoint/pallas_call | solution.py:254
  50.9 1.6 %copy.7 = f32[2,64,256]{2,1,0:T(8,128)} copy(f32[2,64,256]{2,1,0:T(8,128)} %get-tuple-element.4) | data formatting | bytes 262144
  52.4 1.6 %copy.8 = f32[2,64,256]{2,1,0:T(8,128)} copy(f32[2,64,256]{2,1,0:T(8,128)} %get-tuple-element.5) | data formatting | bytes 262144

commit v2 on v1

v2 whole, which is shorter than its diff:
```python
import jax
import jax.numpy as jnp
from jax import lax
from jax.experimental import pallas as pl
from jax.experimental.pallas import tpu as pltpu
from jax.sharding import PartitionSpec as P

MESH = pl.DeviceIdType.MESH
F32 = jnp.float32

STRIPS = 64
LAGS = 4
NK = 32
PAIRS = NK // 2
ROWS = 64
NX = 1024
XB = NX // 128
COLS = NX // STRIPS
PADL = 16
PADX = 136
PADF = 72
SLOT = 80
OUTX = NX // LAGS
SUB = 128
SUBX = SUB + 8
EXP = 80
CHUNKS = 8
KC = NK // CHUNKS


def copy_bytes(ref, sem):
    return pltpu.make_async_copy(ref, ref, sem)


def kernel(
    grad, source, receiver, out_s, out_r,
    edge, tiles, filt, packed, raw, land, field, halo_out, halo_in,
    sums, part, relay, near_in, own,
    edge_sem, raw_sem, load_sem, a2a_send, a2a_recv,
    halo_send, halo_recv, rs_send, rs_recv,
):
    me = lax.axis_index("strip")
    lag = lax.axis_index("lag")
    up_lag = lax.rem(lag + 1, LAGS)
    down_lag = lax.rem(lag + LAGS - 1, LAGS)
    next_strip = lax.rem(me + 1, STRIPS)
    prev_strip = lax.rem(me + STRIPS - 1, STRIPS)
    my_y, my_x, my_z, my_core = me // 16, (me // 4) % 4, (me // 2) % 2, me % 2

    def peer(i):
        y = lax.rem(my_y + i // 16, 4)
        x = lax.rem(my_x + (i // 4) % 4, 4)
        z = lax.rem(my_z + (i // 2) % 2, 2)
        core = lax.rem(my_core + i % 2, 2)
        return ((y * 4 + x) * 2 + z) * 2 + core, (i // 2) % 2, core

    def sender_lag(cross, core):
        side = lax.rem(lag + LAGS - 1 + 2 * my_z, LAGS)
        return jnp.where(cross * core == 1, side, lag)

    def target_lag(cross):
        side = lax.rem(lag + LAGS - 1 + 2 * my_z, LAGS)
        return jnp.where(cross * my_core == 1, side, lag)

    barrier = pltpu.get_barrier_semaphore()

    def greet(i, carry):
        strip, cross, core = peer(i)
        pl.semaphore_signal(
            barrier, inc=1, device_id=(strip, sender_lag(cross, core)), device_id_type=MESH
        )
        return carry

    for other in (up_lag, down_lag):
        pl.semaphore_signal(barrier, inc=1, device_id=(me, other), device_id_type=MESH)
    for other in (next_strip, prev_strip):
        pl.semaphore_signal(barrier, inc=1, device_id=(other, lag), device_id_type=MESH)
    lax.fori_loop(1, STRIPS, greet, 0)

    pltpu.make_async_copy(receiver, raw.at[1], raw_sem.at[1]).start()
    for b in range(XB):
        lanes = pl.ds(128 * b, 128)
        pltpu.make_async_copy(grad.at[:, 0:8, lanes], edge.at[0, :, b], edge_sem).start()
        pltpu.make_async_copy(
            grad.at[:, ROWS - 8 : ROWS, lanes], edge.at[1, :, b], edge_sem
        ).start()
    pltpu.make_async_copy(source, raw.at[0], raw_sem.at[0]).start()
    for c in range(CHUNKS):
        for b in range(XB):
            pltpu.make_async_copy(
                grad.at[c * KC : (c + 1) * KC, :, 128 * b : 128 * (b + 1)],
                tiles.at[c * KC : (c + 1) * KC, b, 8 : 8 + ROWS, :],
                load_sem.at[c],
            ).start()

    low = lax.broadcasted_iota(jnp.int32, (COLS, 128), 1) < ROWS

    def pack(f):
        def one(j, carry):
            lanes = pl.ds(pl.multiple_of(128 * j, 128), 128)
            first = raw[f, 0, :, lanes]
            second = raw[f, 1, :, lanes]
            packed[f, 2 * j] = jnp.where(low, first, pltpu.roll(second, ROWS, 1))
            packed[f, 2 * j + 1] = jnp.where(low, pltpu.roll(first, ROWS, 1), second)
            return carry

        copy_bytes(raw.at[f], raw_sem.at[f]).wait()
        lax.fori_loop(0, STRIPS // 2, one, 0, unroll=4)

    pack(1)

    copy_bytes(edge, edge_sem).wait()
    flat = edge.reshape(2 * NK * XB * 8, 128)
    halo_out[0] = flat[pl.ds(0, NK * XB, stride=8), :]
    halo_out[1] = flat[pl.ds(NK * XB * 8 + 7, NK * XB, stride=8), :]

    here = pl.ds(pl.multiple_of(PADL + COLS * me, 8), COLS)

    def send_field(f):
        def send(i, carry):
            strip, cross, core = peer(i)
            pltpu.make_async_remote_copy(
                packed.at[f, strip], land.at[f, here, :], a2a_send.at[f], a2a_recv.at[f],
                device_id=(strip, target_lag(cross)), device_id_type=MESH,
            ).start()
            return carry

        lax.fori_loop(1, STRIPS, send, 0)

    pl.semaphore_wait(barrier, STRIPS - 1 + 4)

    halo_up = pltpu.make_async_remote_copy(
        halo_out.at[1], halo_in.at[0], halo_send.at[0], halo_recv.at[0],
        device_id=(next_strip, lag), device_id_type=MESH,
    )
    halo_down = pltpu.make_async_remote_copy(
        halo_out.at[0], halo_in.at[1], halo_send.at[1], halo_recv.at[1],
        device_id=(prev_strip, lag), device_id_type=MESH,
    )
    halo_up.start()
    halo_down.start()
    send_field(1)
    pack(0)
    send_field(0)

    for f in range(2):
        land[f, 0:PADL, :] = jnp.zeros((PADL, 128), F32)
        land[f, PADL + NX :, :] = jnp.zeros((PADL, 128), F32)
        land[f, here, :] = packed[f, me]
        for t in range(2):
            field[f, t, 0:PADX, :] = jnp.zeros((PADX, 128), F32)
            field[f, t, PADX + NX :, :] = jnp.zeros((PADX, 128), F32)
    filt[0:PADF, :] = jnp.zeros((PADF, 128), F32)
    filt[PADF + PAIRS * NX :, :] = jnp.zeros((PADF, 128), F32)

    halo_up.wait()
    halo_down.wait()
    halo_in[0] = jnp.where(me == 0, 0.0, halo_in[0])
    halo_in[1] = jnp.where(me == STRIPS - 1, 0.0, halo_in[1])

    lane = lax.broadcasted_iota(jnp.int32, (ROWS, 128), 1)

    def filtered(k):
        for b in range(XB):
            tiles[k, b, 7:8, :] = halo_in[0, pl.ds(k * XB + b, 1), :]
            tiles[k, b, 8 + ROWS : 9 + ROWS, :] = halo_in[1, pl.ds(k * XB + b, 1), :]
        centers = [tiles[k, b, 8 : 8 + ROWS, :] for b in range(XB)]
        lefts = [pltpu.roll(c, 1, 1) for c in centers]
        rights = [pltpu.roll(c, 127, 1) for c in centers]
        none = jnp.zeros((ROWS, 128), F32)
        out = []
        for b in range(XB):
            above = tiles[k, b, 7 : 7 + ROWS, :]
            below = tiles[k, b, 9 : 9 + ROWS, :]
            left = jnp.where(lane == 0, lefts[b - 1] if b else none, lefts[b])
            right = jnp.where(lane == 127, rights[b + 1] if b < XB - 1 else none, rights[b])
            out.append(8.0 * centers[b] - ((above + below) + (left + right)))
        return out

    def pair(p, carry):
        one = filtered(2 * p)
        two = filtered(2 * p + 1)
        for b in range(XB):
            base = pl.multiple_of(PADF + p * NX + 128 * b, 8)
            filt[pl.ds(base, 128), :] = jnp.concatenate([one[b], two[b]], axis=0).T
        return carry

    for c in range(CHUNKS):
        copy_bytes(tiles.at[c * KC : (c + 1) * KC, :, 8 : 8 + ROWS, :], load_sem.at[c]).wait()
        lax.fori_loop(c * KC // 2, (c + 1) * KC // 2, pair, 0)

    first_lag = lag * NK - NK * LAGS // 2

    def lag_copy(n, src, dst, to):
        return pltpu.make_async_remote_copy(
            src, dst, rs_send.at[n], rs_recv.at[n], device_id=(me, to), device_id_type=MESH
        )

    def adjoint(f):
        sign = 1 if f == 1 else -1
        copy_bytes(packed.at[f, 0 : STRIPS - 1], a2a_recv.at[f]).wait()

        wide = lax.broadcasted_iota(jnp.int32, (EXP, 128), 1) < ROWS

        def expand(i, carry):
            at = pl.multiple_of(PADL - 8 + i * EXP, 8)
            this = land[f, pl.ds(at, EXP), :]
            other = land[f, pl.ds(at + sign, EXP), :]
            to = pl.ds(pl.multiple_of(PADX - 8 + i * EXP, 8), EXP)
            field[f, 0, to, :] = jnp.where(wide, this, pltpu.roll(other, ROWS, 1))
            field[f, 1, to, :] = jnp.where(wide, pltpu.roll(this, ROWS, 1), other)
            return carry

        lax.fori_loop(0, (NX + 16) // EXP, expand, 0)

        half = lax.broadcasted_iota(jnp.int32, (SUB, 128), 1) < ROWS
        start = 0 if sign == 1 else -8

        def products(block, i, out):
            x = block * OUTX + i * SUB + start

            def step(p, totals):
                h = (first_lag + 2 * p) * sign
                g = filt[pl.ds(PADF + p * NX + x + h, SUBX), :]
                rows = pl.ds(PADX + x + 2 * h, SUBX)
                return totals[0] + g * field[f, 0, rows, :], totals[1] + g * field[f, 1, rows, :]

            zero = jnp.zeros((SUBX, 128), F32)
            a, b = lax.fori_loop(0, PAIRS, step, (zero, zero), unroll=2)
            sums[0] = a
            sums[1] = b
            own_at = 0 if sign == 1 else 8
            a, b = sums[0, own_at : own_at + SUB], sums[1, own_at : own_at + SUB]
            own_at += sign
            c, d = sums[0, own_at : own_at + SUB], sums[1, own_at : own_at + SUB]
            out[...] = jnp.where(half, a, pltpu.roll(b, ROWS, 1)) + jnp.where(
                half, pltpu.roll(c, ROWS, 1), d
            )

        far = lax.rem(lag + 2, LAGS)
        products(far, 0, part.at[f, 0, 0])
        far_up = lag_copy(6 * f, part.at[f, 0, 0], relay.at[f, 0], up_lag)
        far_up.start()
        products(far, 1, part.at[f, 0, 1])
        far_down = lag_copy(6 * f + 1, part.at[f, 0, 1], relay.at[f, 1], down_lag)
        far_down.start()
        products(up_lag, 1, part.at[f, 1, 1])
        up_1 = lag_copy(6 * f + 2, part.at[f, 1, 1], near_in.at[f, 0, 1], up_lag)
        up_1.start()
        products(down_lag, 0, part.at[f, 2, 0])
        down_0 = lag_copy(6 * f + 3, part.at[f, 2, 0], near_in.at[f, 1, 0], down_lag)
        down_0.start()
        products(up_lag, 0, part.at[f, 1, 0])
        products(down_lag, 1, part.at[f, 2, 1])
        products(lag, 0, own.at[f, 0])
        products(lag, 1, own.at[f, 1])
        far_up.wait_recv()
        part[f, 1, 0] = part[f, 1, 0] + relay[f, 0]
        up_0 = lag_copy(6 * f + 4, part.at[f, 1, 0], near_in.at[f, 0, 0], up_lag)
        up_0.start()
        far_down.wait_recv()
        part[f, 2, 1] = part[f, 2, 1] + relay[f, 1]
        down_1 = lag_copy(6 * f + 5, part.at[f, 2, 1], near_in.at[f, 1, 1], down_lag)
        down_1.start()
        return far_up, far_down, up_1, down_0, up_0, down_1

    def finish(f, out, copies):
        far_up, far_down, up_1, down_0, up_0, down_1 = copies
        for copy in (up_1, down_0, up_0, down_1):
            copy.wait_recv()
        for b in range(OUTX // 128):
            total = own[f, b] + near_in[f, 0, b] + near_in[f, 1, b]
            turned = (0.25 * total).T
            lanes = pl.ds(128 * b, 128)
            out[0, :, lanes] = turned[0:ROWS]
            out[1, :, lanes] = turned[ROWS:]

    copies_s = adjoint(1)
    copies_r = adjoint(0)
    finish(1, out_s, copies_s)
    finish(0, out_r, copies_r)

    for copy in copies_s + copies_r:
        copy.wait_send()
    for f in range(2):
        copy_bytes(packed.at[f, 0 : STRIPS - 1], a2a_send.at[f]).wait()


def local(image_grad, source_field, receiver_field):
    vmem = pltpu.VMEM
    dma = pltpu.SemaphoreType.DMA
    out = jax.ShapeDtypeStruct((2, ROWS, OUTX), F32)
    return pl.pallas_call(
        kernel,
        out_shape=(out, out),
        in_specs=[pl.BlockSpec(memory_space=pl.ANY)] * 3,
        out_specs=[pl.BlockSpec(memory_space=pltpu.VMEM)] * 2,
        scratch_shapes=[
            vmem((2, NK, XB, 8, 128), F32),
            vmem((NK, XB, SLOT, 128), F32),
            vmem((PAIRS * NX + 2 * PADF, 128), F32),
            vmem((2, STRIPS, COLS, 128), F32),
            vmem((2, 2, COLS, STRIPS * ROWS), F32),
            vmem((2, NX + 2 * PADL, 128), F32),
            vmem((2, 2, NX + 2 * PADX, 128), F32),
            vmem((2, NK * XB, 128), F32),
            vmem((2, NK * XB, 128), F32),
            vmem((2, SUBX, 128), F32),
            vmem((2, 3, 2, SUB, 128), F32),
            vmem((2, 2, SUB, 128), F32),
            vmem((2, 2, 2, SUB, 128), F32),
            vmem((2, 2, SUB, 128), F32),
            dma,
            dma((2,)),
            dma((CHUNKS,)),
            dma((2,)),
            dma((2,)),
            dma((2,)),
            dma((2,)),
            dma((12,)),
            dma((12,)),
        ],
        compiler_params=pltpu.CompilerParams(
            collective_id=0, has_side_effects=True, vmem_limit_bytes=60 << 20
        ),
        name="adjoint",
    )(image_grad, jnp.swapaxes(source_field, 1, 2), jnp.swapaxes(receiver_field, 1, 2))


def solution(mesh):
    in_specs = (P("lag", "strip", None), P(None, None, "strip"), P(None, None, "strip"))
    out_specs = (P(None, "strip", "lag"), P(None, "strip", "lag"))
    return jax.shard_map(local, mesh=mesh, in_specs=in_specs, out_specs=out_specs, check_vma=False)
```

time: 54.1 us -> 53 us (0.980)
  Pallas kernels: 50.2 us -> 49 us
    pallas_call x1, Pallas kernels: 50.2 us -> 49 us  [local(): pl.pallas_call(kernel, out_shape=(out, out), in_specs=[pl.BlockSpec(memor...]
where the time goes in v2:
time: 53 us; the launch traced here: 52.8 us
  Pallas kernels  49 us (92%)
  local copies, waits for them, and re-layouts  3.14 us (6%)
  between operations  0.64 us (1%)
    pallas_call x1, Pallas kernels, local(): pl.pallas_call(kernel, out_shape=(out, out), in_specs=[pl.BlockSpec(memor...  49 us
    unnamed x2, local copies, waits for them, and re-layouts  3.14 us

profile of v2, /device:TPU:1, one launch (start us, length us, event | category | flops | bytes accessed | tf_op | source)
XLA Modules:
  0.0 52.8 jit_solution(1462628074293343120)
XLA Ops:
  0.6 49.0 %adjoint.1 = (f32[2,64,256]{2,1,0:T(8,128)}, f32[2,64,256]{2,1,0:T(8,128)}) custom-call(f32[32,64,1024]{2,1,0:T(8,128)} %grad.1, f32[2,16,4096]{2,1,0:T(8,128)} %bitcast.2, f32[2,16,4096]{2,1,0:T(8,128)} %bitcast.3), custom_call_target="tpu_custom_call" | custom-call | tf_op jit(solution)/shard_map/adjoint/pallas_call | solution.py:293
  49.6 1.6 %copy.7 = f32[2,64,256]{2,1,0:T(8,128)} copy(f32[2,64,256]{2,1,0:T(8,128)} %get-tuple-element.4) | data formatting | bytes 262144
  51.2 1.6 %copy.8 = f32[2,64,256]{2,1,0:T(8,128)} copy(f32[2,64,256]{2,1,0:T(8,128)} %get-tuple-element.5) | data formatting | bytes 262144

commit v3 on v2

--- a/solution.py
+++ b/solution.py
@@ -34,7 +34,7 @@
 
 def kernel(
     grad, source, receiver, out_s, out_r,
-    edge, tiles, filt, packed, raw, land, field, halo_out, halo_in,
+    edge, tiles, smooth, columns, filt, packed, raw, land, field, halo_out, halo_in,
     sums, part, relay, near_in, own,
     edge_sem, raw_sem, load_sem, a2a_send, a2a_recv,
     halo_send, halo_recv, rs_send, rs_recv,
@@ -45,37 +45,38 @@
     down_lag = lax.rem(lag + LAGS - 1, LAGS)
     next_strip = lax.rem(me + 1, STRIPS)
     prev_strip = lax.rem(me + STRIPS - 1, STRIPS)
-    my_y, my_x, my_z, my_core = me // 16, (me // 4) % 4, (me // 2) % 2, me % 2
-
-    def peer(i):
-        y = lax.rem(my_y + i // 16, 4)
-        x = lax.rem(my_x + (i // 4) % 4, 4)
-        z = lax.rem(my_z + (i // 2) % 2, 2)
-        core = lax.rem(my_core + i % 2, 2)
-        return ((y * 4 + x) * 2 + z) * 2 + core, (i // 2) % 2, core
-
-    def sender_lag(cross, core):
-        side = lax.rem(lag + LAGS - 1 + 2 * my_z, LAGS)
-        return jnp.where(cross * core == 1, side, lag)
-
-    def target_lag(cross):
-        side = lax.rem(lag + LAGS - 1 + 2 * my_z, LAGS)
-        return jnp.where(cross * my_core == 1, side, lag)
+    chip, my_z, my_core = lax.div(me, 4), lax.rem(lax.div(me, 2), 2), lax.rem(me, 2)
+
+    side = lax.rem(lag + LAGS - 1 + 2 * my_z, LAGS)
+    crossing = [jnp.where(my_z == z, lag, side) for z in range(2)]
+    sender_lag = [lag, crossing[0], lag, crossing[1]]
+    target_lag = [jnp.where(my_core == 1, crossing[e // 2], lag) for e in range(4)]
+
+    def each_peer(lags, act):
+        def others(j, carry):
+            base = lax.rem(chip + j, STRIPS // 4) * 4
+            for e in range(4):
+                act(base + e, lags[e])
+            return carry
+
+        lax.fori_loop(1, STRIPS // 4, others, 0)
+        for e in range(1, 4):
+            place = lax.rem(lax.rem(me, 4) + e, 4)
+            to = lags[0]
+            for n in range(1, 4):
+                to = jnp.where(place == n, lags[n], to)
+            act(chip * 4 + place, to)
 
     barrier = pltpu.get_barrier_semaphore()
 
-    def greet(i, carry):
-        strip, cross, core = peer(i)
-        pl.semaphore_signal(
-            barrier, inc=1, device_id=(strip, sender_lag(cross, core)), device_id_type=MESH
-        )
-        return carry
-
+    def greet(strip, to):
+        pl.semaphore_signal(barrier, inc=1, device_id=(strip, to), device_id_type=MESH)
+
+    each_peer(sender_lag, greet)
     for other in (up_lag, down_lag):
-        pl.semaphore_signal(barrier, inc=1, device_id=(me, other), device_id_type=MESH)
+        greet(me, other)
     for other in (next_strip, prev_strip):
-        pl.semaphore_signal(barrier, inc=1, device_id=(other, lag), device_id_type=MESH)
-    lax.fori_loop(1, STRIPS, greet, 0)
+        greet(other, lag)
 
     pltpu.make_async_copy(receiver, raw.at[1], raw_sem.at[1]).start()
     for b in range(XB):
@@ -85,11 +86,12 @@
             grad.at[:, ROWS - 8 : ROWS, lanes], edge.at[1, :, b], edge_sem
         ).start()
     pltpu.make_async_copy(source, raw.at[0], raw_sem.at[0]).start()
+    by_lag = tiles.reshape(NK, XB, SLOT, 128)
     for c in range(CHUNKS):
         for b in range(XB):
             pltpu.make_async_copy(
                 grad.at[c * KC : (c + 1) * KC, :, 128 * b : 128 * (b + 1)],
-                tiles.at[c * KC : (c + 1) * KC, b, 8 : 8 + ROWS, :],
+                by_lag.at[c * KC : (c + 1) * KC, b, 8 : 8 + ROWS, :],
                 load_sem.at[c],
             ).start()
 
@@ -117,15 +119,13 @@
     here = pl.ds(pl.multiple_of(PADL + COLS * me, 8), COLS)
 
     def send_field(f):
-        def send(i, carry):
-            strip, cross, core = peer(i)
+        def send(strip, to):
             pltpu.make_async_remote_copy(
                 packed.at[f, strip], land.at[f, here, :], a2a_send.at[f], a2a_recv.at[f],
-                device_id=(strip, target_lag(cross)), device_id_type=MESH,
+                device_id=(strip, to), device_id_type=MESH,
             ).start()
-            return carry
-
-        lax.fori_loop(1, STRIPS, send, 0)
+
+        each_peer(target_lag, send)
 
     pl.semaphore_wait(barrier, STRIPS - 1 + 4)
 
@@ -153,41 +153,48 @@
     filt[0:PADF, :] = jnp.zeros((PADF, 128), F32)
     filt[PADF + PAIRS * NX :, :] = jnp.zeros((PADF, 128), F32)
 
+    tile_rows = tiles.reshape(NK * XB * SLOT, 128)
+    blank = jnp.zeros((NK * XB, 128), F32)
+    for row in (7, 8 + ROWS):
+        tile_rows[pl.ds(row, NK * XB, stride=SLOT), :] = blank
+
+    def prepare(p, carry):
+        columns[p, 0:8, :] = jnp.zeros((8, 128), F32)
+        columns[p, 8 + NX :, :] = jnp.zeros((8, 128), F32)
+        for b in range(XB):
+            centers = []
+            for n in range(2):
+                j = (2 * p + n) * XB + b
+                center = tiles[j, 8 : 8 + ROWS, :]
+                above = tiles[j, 7 : 7 + ROWS, :]
+                below = tiles[j, 9 : 9 + ROWS, :]
+                smooth[j] = 8.0 * center - (above + below)
+                centers.append(center)
+            columns[p, 8 + 128 * b : 136 + 128 * b, :] = jnp.concatenate(centers, axis=0).T
+        return carry
+
+    for c in range(CHUNKS):
+        at = pl.ds(c * KC * XB, KC * XB)
+        copy_bytes(tiles.at[at, 8 : 8 + ROWS, :], load_sem.at[c]).wait()
+        lax.fori_loop(c * KC // 2, (c + 1) * KC // 2, prepare, 0)
+
     halo_up.wait()
     halo_down.wait()
-    halo_in[0] = jnp.where(me == 0, 0.0, halo_in[0])
-    halo_in[1] = jnp.where(me == STRIPS - 1, 0.0, halo_in[1])
-
-    lane = lax.broadcasted_iota(jnp.int32, (ROWS, 128), 1)
-
-    def filtered(k):
+    smooth_rows = smooth.reshape(NK * XB * ROWS, 128)
+    first = pl.ds(0, NK * XB, stride=ROWS)
+    last = pl.ds(ROWS - 1, NK * XB, stride=ROWS)
+    smooth_rows[first, :] = smooth_rows[first, :] - jnp.where(me == 0, 0.0, halo_in[0])
+    smooth_rows[last, :] = smooth_rows[last, :] - jnp.where(me == STRIPS - 1, 0.0, halo_in[1])
+
+    def turn(p, carry):
         for b in range(XB):
-            tiles[k, b, 7:8, :] = halo_in[0, pl.ds(k * XB + b, 1), :]
-            tiles[k, b, 8 + ROWS : 9 + ROWS, :] = halo_in[1, pl.ds(k * XB + b, 1), :]
-        centers = [tiles[k, b, 8 : 8 + ROWS, :] for b in range(XB)]
-        lefts = [pltpu.roll(c, 1, 1) for c in centers]
-        rights = [pltpu.roll(c, 127, 1) for c in centers]
-        none = jnp.zeros((ROWS, 128), F32)
-        out = []
-        for b in range(XB):
-            above = tiles[k, b, 7 : 7 + ROWS, :]
-            below = tiles[k, b, 9 : 9 + ROWS, :]
-            left = jnp.where(lane == 0, lefts[b - 1] if b else none, lefts[b])
-            right = jnp.where(lane == 127, rights[b + 1] if b < XB - 1 else none, rights[b])
-            out.append(8.0 * centers[b] - ((above + below) + (left + right)))
-        return out
-
-    def pair(p, carry):
-        one = filtered(2 * p)
-        two = filtered(2 * p + 1)
-        for b in range(XB):
+            both = [smooth[(2 * p + n) * XB + b] for n in range(2)]
+            sides = columns[p, 7 + 128 * b : 135 + 128 * b, :] + columns[p, 9 + 128 * b : 137 + 128 * b, :]
             base = pl.multiple_of(PADF + p * NX + 128 * b, 8)
-            filt[pl.ds(base, 128), :] = jnp.concatenate([one[b], two[b]], axis=0).T
+            filt[pl.ds(base, 128), :] = jnp.concatenate(both, axis=0).T - sides
         return carry
 
-    for c in range(CHUNKS):
-        copy_bytes(tiles.at[c * KC : (c + 1) * KC, :, 8 : 8 + ROWS, :], load_sem.at[c]).wait()
-        lax.fori_loop(c * KC // 2, (c + 1) * KC // 2, pair, 0)
+    lax.fori_loop(0, PAIRS, turn, 0)
 
     first_lag = lag * NK - NK * LAGS // 2
 
@@ -196,7 +203,7 @@
             src, dst, rs_send.at[n], rs_recv.at[n], device_id=(me, to), device_id_type=MESH
         )
 
-    def adjoint(f):
+    def adjoint(f, between):
         sign = 1 if f == 1 else -1
         copy_bytes(packed.at[f, 0 : STRIPS - 1], a2a_recv.at[f]).wait()
 
@@ -226,7 +233,7 @@
                 return totals[0] + g * field[f, 0, rows, :], totals[1] + g * field[f, 1, rows, :]
 
             zero = jnp.zeros((SUBX, 128), F32)
-            a, b = lax.fori_loop(0, PAIRS, step, (zero, zero), unroll=2)
+            a, b = lax.fori_loop(0, PAIRS, step, (zero, zero), unroll=4)
             sums[0] = a
             sums[1] = b
             own_at = 0 if sign == 1 else 8
@@ -244,6 +251,7 @@
         products(far, 1, part.at[f, 0, 1])
         far_down = lag_copy(6 * f + 1, part.at[f, 0, 1], relay.at[f, 1], down_lag)
         far_down.start()
+        between()
         products(up_lag, 1, part.at[f, 1, 1])
         up_1 = lag_copy(6 * f + 2, part.at[f, 1, 1], near_in.at[f, 0, 1], up_lag)
         up_1.start()
@@ -254,15 +262,18 @@
         products(down_lag, 1, part.at[f, 2, 1])
         products(lag, 0, own.at[f, 0])
         products(lag, 1, own.at[f, 1])
+        up_0 = lag_copy(6 * f + 4, part.at[f, 1, 0], near_in.at[f, 0, 0], up_lag)
+        down_1 = lag_copy(6 * f + 5, part.at[f, 2, 1], near_in.at[f, 1, 1], down_lag)
+        return far_up, far_down, up_1, down_0, up_0, down_1
+
+    def pass_on(f, copies):
+        far_up, far_down, _, _, up_0, down_1 = copies
         far_up.wait_recv()
         part[f, 1, 0] = part[f, 1, 0] + relay[f, 0]
-        up_0 = lag_copy(6 * f + 4, part.at[f, 1, 0], near_in.at[f, 0, 0], up_lag)
         up_0.start()
         far_down.wait_recv()
         part[f, 2, 1] = part[f, 2, 1] + relay[f, 1]
-        down_1 = lag_copy(6 * f + 5, part.at[f, 2, 1], near_in.at[f, 1, 1], down_lag)
         down_1.start()
-        return far_up, far_down, up_1, down_0, up_0, down_1
 
     def finish(f, out, copies):
         far_up, far_down, up_1, down_0, up_0, down_1 = copies
@@ -275,8 +286,9 @@
             out[0, :, lanes] = turned[0:ROWS]
             out[1, :, lanes] = turned[ROWS:]
 
-    copies_s = adjoint(1)
-    copies_r = adjoint(0)
+    copies_s = adjoint(1, lambda: None)
+    copies_r = adjoint(0, lambda: pass_on(1, copies_s))
+    pass_on(0, copies_r)
     finish(1, out_s, copies_s)
     finish(0, out_r, copies_r)
 
@@ -297,7 +309,9 @@
         out_specs=[pl.BlockSpec(memory_space=pltpu.VMEM)] * 2,
         scratch_shapes=[
             vmem((2, NK, XB, 8, 128), F32),
-            vmem((NK, XB, SLOT, 128), F32),
+            vmem((NK * XB, SLOT, 128), F32),
+            vmem((NK * XB, ROWS, 128), F32),
+            vmem((PAIRS, NX + 16, 128), F32),
             vmem((PAIRS * NX + 2 * PADF, 128), F32),
             vmem((2, STRIPS, COLS, 128), F32),
             vmem((2, 2, COLS, STRIPS * ROWS), F32),

time: 53 us -> 50.7 us (0.957)
  Pallas kernels: 49 us -> 46.8 us
    pallas_call x1, Pallas kernels: 49 us -> 46.8 us  [local(): pl.pallas_call(kernel, out_shape=(out, out), in_specs=[pl.BlockSpec(memor...]
where the time goes in v3:
time: 50.7 us; the launch traced here: 50.6 us
  Pallas kernels  46.8 us (92%)
  local copies, waits for them, and re-layouts  3.14 us (6%)
  between operations  0.64 us (1%)
    pallas_call x1, Pallas kernels, local(): pl.pallas_call(kernel, out_shape=(out, out), in_specs=[pl.BlockSpec(memor...  46.8 us
    unnamed x2, local copies, waits for them, and re-layouts  3.14 us

profile of v3, /device:TPU:1, one launch (start us, length us, event | category | flops | bytes accessed | tf_op | source)
XLA Modules:
  0.0 50.6 jit_solution(4793850554620322963)
XLA Ops:
  0.6 46.8 %adjoint.1 = (f32[2,64,256]{2,1,0:T(8,128)}, f32[2,64,256]{2,1,0:T(8,128)}) custom-call(f32[32,64,1024]{2,1,0:T(8,128)} %grad.1, f32[2,16,4096]{2,1,0:T(8,128)} %bitcast.2, f32[2,16,4096]{2,1,0:T(8,128)} %bitcast.3), custom_call_target="tpu_custom_call" | custom-call | tf_op jit(solution)/shard_map/adjoint/pallas_call | solution.py:305
  47.5 1.6 %copy.7 = f32[2,64,256]{2,1,0:T(8,128)} copy(f32[2,64,256]{2,1,0:T(8,128)} %get-tuple-element.4) | data formatting | bytes 262144
  49.0 1.6 %copy.8 = f32[2,64,256]{2,1,0:T(8,128)} copy(f32[2,64,256]{2,1,0:T(8,128)} %get-tuple-element.5) | data formatting | bytes 262144

commit v4 on v3

--- a/solution.py
+++ b/solution.py
@@ -24,7 +24,8 @@
 SUB = 128
 SUBX = SUB + 8
 EXP = 80
-CHUNKS = 8
+VMEM = 56000000
+CHUNKS = 4
 KC = NK // CHUNKS
 
 
@@ -33,7 +34,7 @@
 
 
 def kernel(
-    grad, source, receiver, out_s, out_r,
+    grad, source, receiver, result,
     edge, tiles, smooth, columns, filt, packed, raw, land, field, halo_out, halo_in,
     sums, part, relay, near_in, own,
     edge_sem, raw_sem, load_sem, a2a_send, a2a_recv,
@@ -72,20 +73,17 @@
     def greet(strip, to):
         pl.semaphore_signal(barrier, inc=1, device_id=(strip, to), device_id_type=MESH)
 
+    pltpu.make_async_copy(receiver, raw.at[1], raw_sem.at[1]).start()
+    pltpu.make_async_copy(grad.at[:, 0:8, :], edge.at[0], edge_sem).start()
+    pltpu.make_async_copy(grad.at[:, ROWS - 8 : ROWS, :], edge.at[1], edge_sem).start()
+    pltpu.make_async_copy(source, raw.at[0], raw_sem.at[0]).start()
+
     each_peer(sender_lag, greet)
     for other in (up_lag, down_lag):
         greet(me, other)
     for other in (next_strip, prev_strip):
         greet(other, lag)
 
-    pltpu.make_async_copy(receiver, raw.at[1], raw_sem.at[1]).start()
-    for b in range(XB):
-        lanes = pl.ds(128 * b, 128)
-        pltpu.make_async_copy(grad.at[:, 0:8, lanes], edge.at[0, :, b], edge_sem).start()
-        pltpu.make_async_copy(
-            grad.at[:, ROWS - 8 : ROWS, lanes], edge.at[1, :, b], edge_sem
-        ).start()
-    pltpu.make_async_copy(source, raw.at[0], raw_sem.at[0]).start()
     by_lag = tiles.reshape(NK, XB, SLOT, 128)
     for c in range(CHUNKS):
         for b in range(XB):
@@ -112,9 +110,9 @@
     pack(1)
 
     copy_bytes(edge, edge_sem).wait()
-    flat = edge.reshape(2 * NK * XB * 8, 128)
-    halo_out[0] = flat[pl.ds(0, NK * XB, stride=8), :]
-    halo_out[1] = flat[pl.ds(NK * XB * 8 + 7, NK * XB, stride=8), :]
+    for n in range(2):
+        for b in range(XB):
+            halo_out[n, b] = edge[n, :, 7 * n, 128 * b : 128 * (b + 1)]
 
     here = pl.ds(pl.multiple_of(PADL + COLS * me, 8), COLS)
 
@@ -181,10 +179,13 @@
     halo_up.wait()
     halo_down.wait()
     smooth_rows = smooth.reshape(NK * XB * ROWS, 128)
-    first = pl.ds(0, NK * XB, stride=ROWS)
-    last = pl.ds(ROWS - 1, NK * XB, stride=ROWS)
-    smooth_rows[first, :] = smooth_rows[first, :] - jnp.where(me == 0, 0.0, halo_in[0])
-    smooth_rows[last, :] = smooth_rows[last, :] - jnp.where(me == STRIPS - 1, 0.0, halo_in[1])
+    for b in range(XB):
+        first = pl.ds(ROWS * b, NK, stride=ROWS * XB)
+        last = pl.ds(ROWS * b + ROWS - 1, NK, stride=ROWS * XB)
+        above = jnp.where(me == 0, 0.0, halo_in[0, b])
+        below = jnp.where(me == STRIPS - 1, 0.0, halo_in[1, b])
+        smooth_rows[first, :] = smooth_rows[first, :] - above
+        smooth_rows[last, :] = smooth_rows[last, :] - below
 
     def turn(p, carry):
         for b in range(XB):
@@ -275,22 +276,17 @@
         part[f, 2, 1] = part[f, 2, 1] + relay[f, 1]
         down_1.start()
 
-    def finish(f, out, copies):
+    def finish(f, copies):
         far_up, far_down, up_1, down_0, up_0, down_1 = copies
         for copy in (up_1, down_0, up_0, down_1):
             copy.wait_recv()
-        for b in range(OUTX // 128):
-            total = own[f, b] + near_in[f, 0, b] + near_in[f, 1, b]
-            turned = (0.25 * total).T
-            lanes = pl.ds(128 * b, 128)
-            out[0, :, lanes] = turned[0:ROWS]
-            out[1, :, lanes] = turned[ROWS:]
+        result[f] = 0.25 * (own[f] + near_in[f, 0] + near_in[f, 1])
 
     copies_s = adjoint(1, lambda: None)
     copies_r = adjoint(0, lambda: pass_on(1, copies_s))
     pass_on(0, copies_r)
-    finish(1, out_s, copies_s)
-    finish(0, out_r, copies_r)
+    finish(1, copies_s)
+    finish(0, copies_r)
 
     for copy in copies_s + copies_r:
         copy.wait_send()
@@ -298,17 +294,25 @@
         copy_bytes(packed.at[f, 0 : STRIPS - 1], a2a_send.at[f]).wait()
 
 
+def turned(result, out_s, out_r):
+    for f, out in ((1, out_s), (0, out_r)):
+        for b in range(OUTX // 128):
+            lanes = pl.ds(128 * b, 128)
+            block = result[f, b].T
+            out[0, :, lanes] = block[0:ROWS]
+            out[1, :, lanes] = block[ROWS:]
+
+
 def local(image_grad, source_field, receiver_field):
     vmem = pltpu.VMEM
     dma = pltpu.SemaphoreType.DMA
-    out = jax.ShapeDtypeStruct((2, ROWS, OUTX), F32)
-    return pl.pallas_call(
+    result = pl.pallas_call(
         kernel,
-        out_shape=(out, out),
-        in_specs=[pl.BlockSpec(memory_space=pl.ANY)] * 3,
-        out_specs=[pl.BlockSpec(memory_space=pltpu.VMEM)] * 2,
+        out_shape=jax.ShapeDtypeStruct((2, OUTX // 128, 128, 128), F32),
+        in_specs=[pl.BlockSpec(memory_space=pltpu.HBM)] * 3,
+        out_specs=pl.BlockSpec(memory_space=pltpu.VMEM),
         scratch_shapes=[
-            vmem((2, NK, XB, 8, 128), F32),
+            vmem((2, NK, 8, NX), F32),
             vmem((NK * XB, SLOT, 128), F32),
             vmem((NK * XB, ROWS, 128), F32),
             vmem((PAIRS, NX + 16, 128), F32),
@@ -317,8 +321,8 @@
             vmem((2, 2, COLS, STRIPS * ROWS), F32),
             vmem((2, NX + 2 * PADL, 128), F32),
             vmem((2, 2, NX + 2 * PADX, 128), F32),
-            vmem((2, NK * XB, 128), F32),
-            vmem((2, NK * XB, 128), F32),
+            vmem((2, XB, NK, 128), F32),
+            vmem((2, XB, NK, 128), F32),
             vmem((2, SUBX, 128), F32),
             vmem((2, 3, 2, SUB, 128), F32),
             vmem((2, 2, SUB, 128), F32),
@@ -335,10 +339,19 @@
             dma((12,)),
         ],
         compiler_params=pltpu.CompilerParams(
-            collective_id=0, has_side_effects=True, vmem_limit_bytes=60 << 20
+            collective_id=0, has_side_effects=True, vmem_limit_bytes=VMEM
         ),
         name="adjoint",
     )(image_grad, jnp.swapaxes(source_field, 1, 2), jnp.swapaxes(receiver_field, 1, 2))
+    out = jax.ShapeDtypeStruct((2, ROWS, OUTX), F32)
+    return pl.pallas_call(
+        turned,
+        out_shape=(out, out),
+        in_specs=[pl.BlockSpec(memory_space=pltpu.VMEM)],
+        out_specs=[pl.BlockSpec(memory_space=pltpu.VMEM)] * 2,
+        compiler_params=pltpu.CompilerParams(vmem_limit_bytes=4 << 20),
+        name="turned",
+    )(result)
 
 
 def solution(mesh):

time: 50.7 us -> 47.5 us (0.937)
  local copies, waits for them, and re-layouts: 3.14 us -> 0 us
    unnamed x2 -> x0, local copies, waits for them, and re-layouts: 3.14 us -> none
    pallas_call x1 -> x2, Pallas kernels: 46.8 us -> 46.8 us  [the longest x1 46 us: local(): pl.pallas_call(kernel, out_shape=jax.ShapeDtypeStruct((2, OUTX // 128, 12...]
where the time goes in v4:
time: 47.5 us; the launch traced here: 47.4 us
  Pallas kernels  46.8 us (99%)
  between operations  0.64 us (1%)
    pallas_call x1, Pallas kernels, local(): pl.pallas_call(kernel, out_shape=jax.ShapeDtypeStruct((2, OUTX // 128, 12...  46 us

profile of v4, /device:TPU:1, one launch (start us, length us, event | category | flops | bytes accessed | tf_op | source)
XLA Modules:
  0.0 47.4 jit_solution(12196802495145078751)
XLA Ops:
  0.6 46.0 %adjoint.1.result = f32[2,2,128,128]{3,2,1,0:T(8,128)S(1)} custom-call(f32[32,64,1024]{2,1,0:T(8,128)} %grad.1, f32[2,16,4096]{2,1,0:T(8,128)} %bitcast.2, f32[2,16,4096]{2,1,0:T(8,128)} %bitcast.3), custom_call_target="tpu_custom_call" | custom-call | tf_op jit(solution)/shard_map/adjoint/pallas_call | solution.py:309
  46.6 0.8 %turned.1 = (f32[2,64,256]{2,1,0:T(8,128)}, f32[2,64,256]{2,1,0:T(8,128)}) custom-call(f32[2,2,128,128]{3,2,1,0:T(8,128)S(1)} %adjoint.1.result), custom_call_target="tpu_custom_call" | custom-call | tf_op jit(solution)/shard_map/turned/pallas_call | solution.py:347

commit v5 on v4

v5 whole, which is shorter than its diff:
```python
import jax
import jax.numpy as jnp
from jax import lax
from jax.experimental import pallas as pl
from jax.experimental.pallas import tpu as pltpu
from jax.sharding import PartitionSpec as P

MESH = pl.DeviceIdType.MESH
F32 = jnp.float32

STRIPS = 64
LAGS = 4
NK = 32
PAIRS = NK // 2
ROWS = 64
NX = 1024
XB = NX // 128
COLS = NX // STRIPS
PADD = 16
PIECE = COLS // 2
PHASES = ((1, 0), (1, 1), (0, 0), (0, 1))
PADX = 136
PADF = 72
SLOT = 80
OUTX = NX // LAGS
SUB = 128
HALF = SUB // 2
SUBX = SUB + 8
EXP = 80
VMEM = 56000000
CHUNKS = 4
KC = NK // CHUNKS


def copy_bytes(ref, sem):
    return pltpu.make_async_copy(ref, ref, sem)


def kernel(
    grad, source, receiver, result,
    edge, tiles, smooth, columns, filt, packed, raw, land, twice, field, halo_out, halo_in,
    sums, part, relay, near_in, own,
    edge_sem, raw_sem, load_sem, a2a_send, a2a_recv,
    halo_send, halo_recv, rs_send, rs_recv,
):
    me = lax.axis_index("strip")
    lag = lax.axis_index("lag")
    up_lag = lax.rem(lag + 1, LAGS)
    down_lag = lax.rem(lag + LAGS - 1, LAGS)
    next_strip = lax.rem(me + 1, STRIPS)
    prev_strip = lax.rem(me + STRIPS - 1, STRIPS)
    chip, my_z, my_core = lax.div(me, 4), lax.rem(lax.div(me, 2), 2), lax.rem(me, 2)

    side = lax.rem(lag + LAGS - 1 + 2 * my_z, LAGS)
    crossing = [jnp.where(my_z == z, lag, side) for z in range(2)]
    sender_lag = [lag, crossing[0], lag, crossing[1]]
    target_lag = [jnp.where(my_core == 1, crossing[e // 2], lag) for e in range(4)]

    def each_peer(lags, act):
        def others(j, carry):
            base = lax.rem(chip + j, STRIPS // 4) * 4
            for e in range(4):
                act(base + e, lags[e])
            return carry

        lax.fori_loop(1, STRIPS // 4, others, 0)
        for e in range(1, 4):
            place = lax.rem(lax.rem(me, 4) + e, 4)
            to = lags[0]
            for n in range(1, 4):
                to = jnp.where(place == n, lags[n], to)
            act(chip * 4 + place, to)

    barrier = pltpu.get_barrier_semaphore()

    def greet(strip, to):
        pl.semaphore_signal(barrier, inc=1, device_id=(strip, to), device_id_type=MESH)

    fields = (source, receiver)
    pltpu.make_async_copy(receiver.at[0], raw.at[0], raw_sem.at[0]).start()
    pltpu.make_async_copy(grad.at[:, 0:8, :], edge.at[0], edge_sem).start()
    pltpu.make_async_copy(grad.at[:, ROWS - 8 : ROWS, :], edge.at[1], edge_sem).start()
    for q, (f, t) in enumerate(PHASES):
        if q:
            pltpu.make_async_copy(fields[f].at[t], raw.at[q], raw_sem.at[q]).start()

    each_peer(sender_lag, greet)
    for other in (up_lag, down_lag):
        greet(me, other)
    for other in (next_strip, prev_strip):
        greet(other, lag)

    by_lag = tiles.reshape(NK, XB, SLOT, 128)
    for c in range(CHUNKS):
        for b in range(XB):
            pltpu.make_async_copy(
                grad.at[c * KC : (c + 1) * KC, :, 128 * b : 128 * (b + 1)],
                by_lag.at[c * KC : (c + 1) * KC, b, 8 : 8 + ROWS, :],
                load_sem.at[c],
            ).start()

    low = lax.broadcasted_iota(jnp.int32, (PIECE, 128), 1) < ROWS

    def pack(q):
        def one(j, carry):
            lanes = pl.ds(pl.multiple_of(128 * j, 128), 128)
            first = raw[q, 0:PIECE, lanes]
            second = raw[q, PIECE:COLS, lanes]
            packed[q, 2 * j] = jnp.where(low, first, pltpu.roll(second, ROWS, 1))
            packed[q, 2 * j + 1] = jnp.where(low, pltpu.roll(first, ROWS, 1), second)
            return carry

        copy_bytes(raw.at[q], raw_sem.at[q]).wait()
        lax.fori_loop(0, STRIPS // 2, one, 0, unroll=8)

    pack(0)

    copy_bytes(edge, edge_sem).wait()
    for n in range(2):
        for b in range(XB):
            halo_out[n, b] = edge[n, :, 7 * n, 128 * b : 128 * (b + 1)]

    here = pl.ds(pl.multiple_of(PIECE * me, 8), PIECE)

    def send_field(q):
        def send(strip, to):
            pltpu.make_async_remote_copy(
                packed.at[q, strip], land.at[q, here, :], a2a_send.at[q], a2a_recv.at[q],
                device_id=(strip, to), device_id_type=MESH,
            ).start()

        each_peer(target_lag, send)

    pl.semaphore_wait(barrier, STRIPS - 1 + 4)

    halo_up = pltpu.make_async_remote_copy(
        halo_out.at[1], halo_in.at[0], halo_send.at[0], halo_recv.at[0],
        device_id=(next_strip, lag), device_id_type=MESH,
    )
    halo_down = pltpu.make_async_remote_copy(
        halo_out.at[0], halo_in.at[1], halo_send.at[1], halo_recv.at[1],
        device_id=(prev_strip, lag), device_id_type=MESH,
    )
    halo_up.start()
    halo_down.start()
    send_field(0)
    pack(1)
    send_field(1)

    for n in range(2):
        rows = pl.ds(n * (PADD + NX), PADD)
        twice[rows, :] = jnp.zeros((PADD, 128), F32)
        rows = pl.ds(n * (PADX + NX), PADX)
        field[rows, :] = jnp.zeros((PADX, 128), F32)
        rows = pl.ds(n * (PADF + PAIRS * NX), PADF)
        filt[rows, :] = jnp.zeros((PADF, 128), F32)

    tile_rows = tiles.reshape(NK * XB * SLOT, 128)
    blank = jnp.zeros((NK * XB, 128), F32)
    for row in (7, 8 + ROWS):
        tile_rows[pl.ds(row, NK * XB, stride=SLOT), :] = blank

    def prepare(p, carry):
        columns[p, 0:8, :] = jnp.zeros((8, 128), F32)
        columns[p, 8 + NX :, :] = jnp.zeros((8, 128), F32)
        for b in range(XB):
            centers = []
            for n in range(2):
                j = (2 * p + n) * XB + b
                center = tiles[j, 8 : 8 + ROWS, :]
                above = tiles[j, 7 : 7 + ROWS, :]
                below = tiles[j, 9 : 9 + ROWS, :]
                smooth[j] = 8.0 * center - (above + below)
                centers.append(center)
            columns[p, 8 + 128 * b : 136 + 128 * b, :] = jnp.concatenate(centers, axis=0).T
        return carry

    for c in range(CHUNKS):
        at = pl.ds(c * KC * XB, KC * XB)
        copy_bytes(tiles.at[at, 8 : 8 + ROWS, :], load_sem.at[c]).wait()
        lax.fori_loop(c * KC // 2, (c + 1) * KC // 2, prepare, 0)

    halo_up.wait()
    halo_down.wait()
    smooth_rows = smooth.reshape(NK * XB * ROWS, 128)
    for b in range(XB):
        first = pl.ds(ROWS * b, NK, stride=ROWS * XB)
        last = pl.ds(ROWS * b + ROWS - 1, NK, stride=ROWS * XB)
        above = jnp.where(me == 0, 0.0, halo_in[0, b])
        below = jnp.where(me == STRIPS - 1, 0.0, halo_in[1, b])
        smooth_rows[first, :] = smooth_rows[first, :] - above
        smooth_rows[last, :] = smooth_rows[last, :] - below

    def turn(p, carry):
        for b in range(XB):
            both = [smooth[(2 * p + n) * XB + b] for n in range(2)]
            sides = columns[p, 7 + 128 * b : 135 + 128 * b, :] + columns[p, 9 + 128 * b : 137 + 128 * b, :]
            base = pl.multiple_of(PADF + p * NX + 128 * b, 8)
            filt[pl.ds(base, 128), :] = jnp.concatenate(both, axis=0).T - sides
        return carry

    lax.fori_loop(0, PAIRS, turn, 0)

    first_lag = lag * NK - NK * LAGS // 2

    def lag_copy(n, src, dst, to):
        return pltpu.make_async_remote_copy(
            src, dst, rs_send.at[n], rs_recv.at[n], device_id=(me, to), device_id_type=MESH
        )

    low_x = lax.broadcasted_iota(jnp.int32, (EXP, 128), 1) < ROWS

    def adjoint(q, between):
        sign = 1 if PHASES[q][0] == 1 else -1
        land[q, here, :] = packed[q, me]
        copy_bytes(packed.at[q, 0 : STRIPS - 1], a2a_recv.at[q]).wait()

        def unfold(s, carry):
            this = land[q, pl.ds(pl.multiple_of(PIECE * s, 8), PIECE), :]
            other = pltpu.roll(this, ROWS, 1)
            at = pl.multiple_of(PADD + COLS * s, 8)
            twice[pl.ds(at, PIECE), :] = jnp.where(low, this, other)
            twice[pl.ds(at + PIECE, PIECE), :] = jnp.where(low, other, this)
            return carry

        lax.fori_loop(0, STRIPS, unfold, 0, unroll=8)

        def expand(i, carry):
            at = pl.multiple_of(PADD - 8 + i * EXP, 8)
            to = pl.ds(pl.multiple_of(PADX - 8 + i * EXP, 8), EXP)
            field[to, :] = jnp.where(low_x, twice[pl.ds(at, EXP), :], twice[pl.ds(at + sign, EXP), :])
            return carry

        lax.fori_loop(0, (NX + 16) // EXP, expand, 0)

        half = lax.broadcasted_iota(jnp.int32, (HALF, 128), 1) < ROWS
        start = 0 if sign == 1 else -8

        def products(block, i, out):
            x = block * OUTX + i * SUB + start

            def step(p, total):
                h = (first_lag + 2 * p) * sign
                g = filt[pl.ds(PADF + p * NX + x + h, SUBX), :]
                return total + g * field[pl.ds(PADX + x + 2 * h, SUBX), :]

            sums[...] = lax.fori_loop(0, PAIRS, step, jnp.zeros((SUBX, 128), F32), unroll=4)
            at = 0 if sign == 1 else 8
            a, b = sums[at : at + HALF], sums[at + HALF : at + SUB]
            at += sign
            c, d = sums[at : at + HALF], sums[at + HALF : at + SUB]
            out[...] = jnp.where(half, a, pltpu.roll(b, ROWS, 1)) + jnp.where(
                half, pltpu.roll(c, ROWS, 1), d
            )

        far = lax.rem(lag + 2, LAGS)
        products(far, 0, part.at[q, 0, 0])
        far_up = lag_copy(6 * q, part.at[q, 0, 0], relay.at[q, 0], up_lag)
        far_up.start()
        products(far, 1, part.at[q, 0, 1])
        far_down = lag_copy(6 * q + 1, part.at[q, 0, 1], relay.at[q, 1], down_lag)
        far_down.start()
        between()
        products(up_lag, 1, part.at[q, 1, 1])
        up_1 = lag_copy(6 * q + 2, part.at[q, 1, 1], near_in.at[q, 0, 1], up_lag)
        up_1.start()
        products(down_lag, 0, part.at[q, 2, 0])
        down_0 = lag_copy(6 * q + 3, part.at[q, 2, 0], near_in.at[q, 1, 0], down_lag)
        down_0.start()
        products(up_lag, 0, part.at[q, 1, 0])
        products(down_lag, 1, part.at[q, 2, 1])
        products(lag, 0, own.at[q, 0])
        products(lag, 1, own.at[q, 1])
        up_0 = lag_copy(6 * q + 4, part.at[q, 1, 0], near_in.at[q, 0, 0], up_lag)
        down_1 = lag_copy(6 * q + 5, part.at[q, 2, 1], near_in.at[q, 1, 1], down_lag)
        return far_up, far_down, up_1, down_0, up_0, down_1

    def pass_on(q, copies):
        far_up, far_down, _, _, up_0, down_1 = copies
        far_up.wait_recv()
        part[q, 1, 0] = part[q, 1, 0] + relay[q, 0]
        up_0.start()
        far_down.wait_recv()
        part[q, 2, 1] = part[q, 2, 1] + relay[q, 1]
        down_1.start()

    def finish(q, copies):
        far_up, far_down, up_1, down_0, up_0, down_1 = copies
        for copy in (up_1, down_0, up_0, down_1):
            copy.wait_recv()
        result[q] = 0.25 * (own[q] + near_in[q, 0] + near_in[q, 1])

    def rest_of_fields():
        for q in (2, 3):
            pack(q)
            send_field(q)

    copies = []
    for q in range(4):
        copies.append(
            adjoint(q, (lambda q=q: pass_on(q - 1, copies[q - 1])) if q else rest_of_fields)
        )
    pass_on(3, copies[3])
    for q in range(4):
        finish(q, copies[q])

    for q in range(4):
        for copy in copies[q]:
            copy.wait_send()
        copy_bytes(packed.at[q, 0 : STRIPS - 1], a2a_send.at[q]).wait()


def turned(result, out_s, out_r):
    for q, (f, t) in enumerate(PHASES):
        out = out_s if f == 1 else out_r
        for b in range(OUTX // SUB):
            block = result[q, b].T
            out[t, :, SUB * b : SUB * (b + 1)] = jnp.concatenate([block[0:ROWS], block[ROWS:]], axis=1)


def local(image_grad, source_field, receiver_field):
    vmem = pltpu.VMEM
    dma = pltpu.SemaphoreType.DMA
    result = pl.pallas_call(
        kernel,
        out_shape=jax.ShapeDtypeStruct((4, OUTX // SUB, HALF, 128), F32),
        in_specs=[pl.BlockSpec(memory_space=pltpu.HBM)] * 3,
        out_specs=pl.BlockSpec(memory_space=pltpu.VMEM),
        scratch_shapes=[
            vmem((2, NK, 8, NX), F32),
            vmem((NK * XB, SLOT, 128), F32),
            vmem((NK * XB, ROWS, 128), F32),
            vmem((PAIRS, NX + 16, 128), F32),
            vmem((PAIRS * NX + 2 * PADF, 128), F32),
            vmem((4, STRIPS, PIECE, 128), F32),
            vmem((4, COLS, STRIPS * ROWS), F32),
            vmem((4, STRIPS * PIECE, 128), F32),
            vmem((NX + 2 * PADD, 128), F32),
            vmem((NX + 2 * PADX, 128), F32),
            vmem((2, XB, NK, 128), F32),
            vmem((2, XB, NK, 128), F32),
            vmem((SUBX, 128), F32),
            vmem((4, 3, 2, HALF, 128), F32),
            vmem((4, 2, HALF, 128), F32),
            vmem((4, 2, 2, HALF, 128), F32),
            vmem((4, 2, HALF, 128), F32),
            dma,
            dma((4,)),
            dma((CHUNKS,)),
            dma((4,)),
            dma((4,)),
            dma((2,)),
            dma((2,)),
            dma((24,)),
            dma((24,)),
        ],
        compiler_params=pltpu.CompilerParams(
            collective_id=0, has_side_effects=True, vmem_limit_bytes=VMEM
        ),
        name="adjoint",
    )(image_grad, jnp.swapaxes(source_field, 1, 2), jnp.swapaxes(receiver_field, 1, 2))
    out = jax.ShapeDtypeStruct((2, ROWS, OUTX), F32)
    return pl.pallas_call(
        turned,
        out_shape=(out, out),
        in_specs=[pl.BlockSpec(memory_space=pltpu.VMEM)],
        out_specs=[pl.BlockSpec(memory_space=pltpu.VMEM)] * 2,
        compiler_params=pltpu.CompilerParams(vmem_limit_bytes=4 << 20),
        name="turned",
    )(result)


def solution(mesh):
    in_specs = (P("lag", "strip", None), P(None, None, "strip"), P(None, None, "strip"))
    out_specs = (P(None, "strip", "lag"), P(None, "strip", "lag"))
    return jax.shard_map(local, mesh=mesh, in_specs=in_specs, out_specs=out_specs, check_vma=False)
```

time: 47.5 us -> 50.8 us (1.069)
  the two profiles are of different devices: /device:TPU:1 before, /device:TPU:8 now
where the time goes in v5:
time: 50.8 us; the launch traced here: 50.7 us
  Pallas kernels  50.1 us (99%)
  between operations  0.64 us (1%)
    pallas_call x1, Pallas kernels, local(): pl.pallas_call(kernel, out_shape=jax.ShapeDtypeStruct((4, OUTX // SUB, HA...  49.1 us

profile of v5, /device:TPU:8, one launch (start us, length us, event | category | flops | bytes accessed | tf_op | source)
XLA Modules:
  0.0 50.7 jit_solution(11471859270090089531)
XLA Ops:
  0.6 49.1 %adjoint.1.result = f32[4,2,64,128]{3,2,1,0:T(8,128)S(1)} custom-call(f32[32,64,1024]{2,1,0:T(8,128)} %grad.1, f32[2,16,4096]{2,1,0:T(8,128)} %bitcast.2, f32[2,16,4096]{2,1,0:T(8,128)} %bitcast.3), custom_call_target="tpu_custom_call" | custom-call | tf_op jit(solution)/shard_map/adjoint/pallas_call | solution.py:324
  49.7 1.0 %turned.1 = (f32[2,64,256]{2,1,0:T(8,128)}, f32[2,64,256]{2,1,0:T(8,128)}) custom-call(f32[4,2,64,128]{3,2,1,0:T(8,128)S(1)} %adjoint.1.result), custom_call_target="tpu_custom_call" | custom-call | tf_op jit(solution)/shard_map/turned/pallas_call | solution.py:363

commit v6 on v5

--- a/solution.py
+++ b/solution.py
@@ -18,6 +18,7 @@
 COLS = NX // STRIPS
 PADD = 16
 PIECE = COLS // 2
+SENDS = (pl.ds(0, 1), pl.ds(1, 1), pl.ds(2, 2))
 PHASES = ((1, 0), (1, 1), (0, 0), (0, 1))
 PADX = 136
 PADF = 72
@@ -122,10 +123,10 @@
 
     here = pl.ds(pl.multiple_of(PIECE * me, 8), PIECE)
 
-    def send_field(q):
+    def send_field(at):
         def send(strip, to):
             pltpu.make_async_remote_copy(
-                packed.at[q, strip], land.at[q, here, :], a2a_send.at[q], a2a_recv.at[q],
+                packed.at[at, strip], land.at[at, here, :], a2a_send.at[at.start], a2a_recv.at[at.start],
                 device_id=(strip, to), device_id_type=MESH,
             ).start()
 
@@ -143,9 +144,9 @@
     )
     halo_up.start()
     halo_down.start()
-    send_field(0)
+    send_field(SENDS[0])
     pack(1)
-    send_field(1)
+    send_field(SENDS[1])
 
     for n in range(2):
         rows = pl.ds(n * (PADD + NX), PADD)
@@ -178,7 +179,11 @@
     for c in range(CHUNKS):
         at = pl.ds(c * KC * XB, KC * XB)
         copy_bytes(tiles.at[at, 8 : 8 + ROWS, :], load_sem.at[c]).wait()
-        lax.fori_loop(c * KC // 2, (c + 1) * KC // 2, prepare, 0)
+        lax.fori_loop(c * KC // 2, (c + 1) * KC // 2, prepare, 0, unroll=2)
+
+    pack(2)
+    pack(3)
+    send_field(SENDS[2])
 
     halo_up.wait()
     halo_down.wait()
@@ -199,7 +204,7 @@
             filt[pl.ds(base, 128), :] = jnp.concatenate(both, axis=0).T - sides
         return carry
 
-    lax.fori_loop(0, PAIRS, turn, 0)
+    lax.fori_loop(0, PAIRS, turn, 0, unroll=2)
 
     first_lag = lag * NK - NK * LAGS // 2
 
@@ -213,7 +218,8 @@
     def adjoint(q, between):
         sign = 1 if PHASES[q][0] == 1 else -1
         land[q, here, :] = packed[q, me]
-        copy_bytes(packed.at[q, 0 : STRIPS - 1], a2a_recv.at[q]).wait()
+        if q < len(SENDS):
+            copy_bytes(packed.at[SENDS[q], 0 : STRIPS - 1], a2a_recv.at[q]).wait()
 
         def unfold(s, carry):
             this = land[q, pl.ds(pl.multiple_of(PIECE * s, 8), PIECE), :]
@@ -290,15 +296,10 @@
             copy.wait_recv()
         result[q] = 0.25 * (own[q] + near_in[q, 0] + near_in[q, 1])
 
-    def rest_of_fields():
-        for q in (2, 3):
-            pack(q)
-            send_field(q)
-
     copies = []
     for q in range(4):
         copies.append(
-            adjoint(q, (lambda q=q: pass_on(q - 1, copies[q - 1])) if q else rest_of_fields)
+            adjoint(q, (lambda q=q: pass_on(q - 1, copies[q - 1])) if q else lambda: None)
         )
     pass_on(3, copies[3])
     for q in range(4):
@@ -307,7 +308,8 @@
     for q in range(4):
         for copy in copies[q]:
             copy.wait_send()
-        copy_bytes(packed.at[q, 0 : STRIPS - 1], a2a_send.at[q]).wait()
+    for n, at in enumerate(SENDS):
+        copy_bytes(packed.at[at, 0 : STRIPS - 1], a2a_send.at[n]).wait()
 
 
 def turned(result, out_s, out_r):
@@ -347,8 +349,8 @@
             dma,
             dma((4,)),
             dma((CHUNKS,)),
-            dma((4,)),
-            dma((4,)),
+            dma((3,)),
+            dma((3,)),
             dma((2,)),
             dma((2,)),
             dma((24,)),

time: 50.8 us -> 47.2 us (0.929)
  the two profiles are of different devices: /device:TPU:8 before, /device:TPU:1 now
where the time goes in v6:
time: 47.2 us; the launch traced here: 47.1 us
  Pallas kernels  46.5 us (99%)
  between operations  0.64 us (1%)
    pallas_call x1, Pallas kernels, local(): pl.pallas_call(kernel, out_shape=jax.ShapeDtypeStruct((4, OUTX // SUB, HA...  45.5 us
    pallas_call x1, Pallas kernels, local(): pl.pallas_call(turned, out_shape=(out, out), in_specs=[pl.BlockSpec(memor...  0.97 us

profile of v6, /device:TPU:1, one launch (start us, length us, event | category | flops | bytes accessed | tf_op | source)
XLA Modules:
  0.0 47.1 jit_solution(9899521703126048114)
XLA Ops:
  0.6 45.5 %adjoint.1.result = f32[4,2,64,128]{3,2,1,0:T(8,128)S(1)} custom-call(f32[32,64,1024]{2,1,0:T(8,128)} %grad.1, f32[2,16,4096]{2,1,0:T(8,128)} %bitcast.2, f32[2,16,4096]{2,1,0:T(8,128)} %bitcast.3), custom_call_target="tpu_custom_call" | custom-call | tf_op jit(solution)/shard_map/adjoint/pallas_call | solution.py:326
  46.2 1.0 %turned.1 = (f32[2,64,256]{2,1,0:T(8,128)}, f32[2,64,256]{2,1,0:T(8,128)}) custom-call(f32[4,2,64,128]{3,2,1,0:T(8,128)S(1)} %adjoint.1.result), custom_call_target="tpu_custom_call" | custom-call | tf_op jit(solution)/shard_map/turned/pallas_call | solution.py:365

commit v7 on v6

--- a/solution.py
+++ b/solution.py
@@ -29,6 +29,7 @@
 SUBX = SUB + 8
 EXP = 80
 VMEM = 56000000
+EARLY = 2
 CHUNKS = 4
 KC = NK // CHUNKS
 
@@ -132,21 +133,8 @@
 
         each_peer(target_lag, send)
 
-    pl.semaphore_wait(barrier, STRIPS - 1 + 4)
-
-    halo_up = pltpu.make_async_remote_copy(
-        halo_out.at[1], halo_in.at[0], halo_send.at[0], halo_recv.at[0],
-        device_id=(next_strip, lag), device_id_type=MESH,
-    )
-    halo_down = pltpu.make_async_remote_copy(
-        halo_out.at[0], halo_in.at[1], halo_send.at[1], halo_recv.at[1],
-        device_id=(prev_strip, lag), device_id_type=MESH,
-    )
-    halo_up.start()
-    halo_down.start()
-    send_field(SENDS[0])
-    pack(1)
-    send_field(SENDS[1])
+    for q in range(1, 4):
+        pack(q)
 
     for n in range(2):
         rows = pl.ds(n * (PADD + NX), PADD)
@@ -176,14 +164,31 @@
             columns[p, 8 + 128 * b : 136 + 128 * b, :] = jnp.concatenate(centers, axis=0).T
         return carry
 
-    for c in range(CHUNKS):
+    def prepare_chunk(c):
         at = pl.ds(c * KC * XB, KC * XB)
         copy_bytes(tiles.at[at, 8 : 8 + ROWS, :], load_sem.at[c]).wait()
         lax.fori_loop(c * KC // 2, (c + 1) * KC // 2, prepare, 0, unroll=2)
 
-    pack(2)
-    pack(3)
-    send_field(SENDS[2])
+    for c in range(EARLY):
+        prepare_chunk(c)
+
+    pl.semaphore_wait(barrier, STRIPS - 1 + 4)
+
+    halo_up = pltpu.make_async_remote_copy(
+        halo_out.at[1], halo_in.at[0], halo_send.at[0], halo_recv.at[0],
+        device_id=(next_strip, lag), device_id_type=MESH,
+    )
+    halo_down = pltpu.make_async_remote_copy(
+        halo_out.at[0], halo_in.at[1], halo_send.at[1], halo_recv.at[1],
+        device_id=(prev_strip, lag), device_id_type=MESH,
+    )
+    halo_up.start()
+    halo_down.start()
+    for at in SENDS:
+        send_field(at)
+
+    for c in range(EARLY, CHUNKS):
+        prepare_chunk(c)
 
     halo_up.wait()
     halo_down.wait()

time: 47.2 us -> 47 us (level)
  no operation moved by 1% of the time
where the time goes in v7:
time: 47 us; the launch traced here: 46.9 us
  Pallas kernels  46.3 us (99%)
  between operations  0.64 us (1%)
    pallas_call x1, Pallas kernels, local(): pl.pallas_call(kernel, out_shape=jax.ShapeDtypeStruct((4, OUTX // SUB, HA...  45.3 us
    pallas_call x1, Pallas kernels, local(): pl.pallas_call(turned, out_shape=(out, out), in_specs=[pl.BlockSpec(memor...  0.97 us

profile of v7, /device:TPU:1, one launch (start us, length us, event | category | flops | bytes accessed | tf_op | source)
XLA Modules:
  0.0 46.9 jit_solution(1565833816607781196)
XLA Ops:
  0.6 45.3 %adjoint.1.result = f32[4,2,64,128]{3,2,1,0:T(8,128)S(1)} custom-call(f32[32,64,1024]{2,1,0:T(8,128)} %grad.1, f32[2,16,4096]{2,1,0:T(8,128)} %bitcast.2, f32[2,16,4096]{2,1,0:T(8,128)} %bitcast.3), custom_call_target="tpu_custom_call" | custom-call | tf_op jit(solution)/shard_map/adjoint/pallas_call | solution.py:331
  46.0 1.0 %turned.1 = (f32[2,64,256]{2,1,0:T(8,128)}, f32[2,64,256]{2,1,0:T(8,128)}) custom-call(f32[4,2,64,128]{3,2,1,0:T(8,128)S(1)} %adjoint.1.result), custom_call_target="tpu_custom_call" | custom-call | tf_op jit(solution)/shard_map/turned/pallas_call | solution.py:370

commit v8 on v6

--- a/solution.py
+++ b/solution.py
@@ -114,6 +114,17 @@
         copy_bytes(raw.at[q], raw_sem.at[q]).wait()
         lax.fori_loop(0, STRIPS // 2, one, 0, unroll=8)
 
+    tile_rows = tiles.reshape(NK * XB * SLOT, 128)
+    for row in (7, 8 + ROWS):
+        tile_rows[pl.ds(row, NK * XB, stride=SLOT), :] = jnp.zeros((NK * XB, 128), F32)
+    for n in range(2):
+        rows = pl.ds(n * (PADD + NX), PADD)
+        twice[rows, :] = jnp.zeros((PADD, 128), F32)
+        rows = pl.ds(n * (PADX + NX), PADX)
+        field[rows, :] = jnp.zeros((PADX, 128), F32)
+        rows = pl.ds(n * (PADF + PAIRS * NX), PADF)
+        filt[rows, :] = jnp.zeros((PADF, 128), F32)
+
     pack(0)
 
     copy_bytes(edge, edge_sem).wait()
@@ -142,24 +153,11 @@
         halo_out.at[0], halo_in.at[1], halo_send.at[1], halo_recv.at[1],
         device_id=(prev_strip, lag), device_id_type=MESH,
     )
+    send_field(SENDS[0])
     halo_up.start()
     halo_down.start()
-    send_field(SENDS[0])
     pack(1)
     send_field(SENDS[1])
-
-    for n in range(2):
-        rows = pl.ds(n * (PADD + NX), PADD)
-        twice[rows, :] = jnp.zeros((PADD, 128), F32)
-        rows = pl.ds(n * (PADX + NX), PADX)
-        field[rows, :] = jnp.zeros((PADX, 128), F32)
-        rows = pl.ds(n * (PADF + PAIRS * NX), PADF)
-        filt[rows, :] = jnp.zeros((PADF, 128), F32)
-
-    tile_rows = tiles.reshape(NK * XB * SLOT, 128)
-    blank = jnp.zeros((NK * XB, 128), F32)
-    for row in (7, 8 + ROWS):
-        tile_rows[pl.ds(row, NK * XB, stride=SLOT), :] = blank
 
     def prepare(p, carry):
         columns[p, 0:8, :] = jnp.zeros((8, 128), F32)
@@ -187,24 +185,38 @@
 
     halo_up.wait()
     halo_down.wait()
-    smooth_rows = smooth.reshape(NK * XB * ROWS, 128)
-    for b in range(XB):
-        first = pl.ds(ROWS * b, NK, stride=ROWS * XB)
-        last = pl.ds(ROWS * b + ROWS - 1, NK, stride=ROWS * XB)
-        above = jnp.where(me == 0, 0.0, halo_in[0, b])
-        below = jnp.where(me == STRIPS - 1, 0.0, halo_in[1, b])
-        smooth_rows[first, :] = smooth_rows[first, :] - above
-        smooth_rows[last, :] = smooth_rows[last, :] - below
-
-    def turn(p, carry):
-        for b in range(XB):
-            both = [smooth[(2 * p + n) * XB + b] for n in range(2)]
-            sides = columns[p, 7 + 128 * b : 135 + 128 * b, :] + columns[p, 9 + 128 * b : 137 + 128 * b, :]
-            base = pl.multiple_of(PADF + p * NX + 128 * b, 8)
-            filt[pl.ds(base, 128), :] = jnp.concatenate(both, axis=0).T - sides
-        return carry
-
-    lax.fori_loop(0, PAIRS, turn, 0, unroll=2)
+    halo_in[0] = jnp.where(me == 0, 0.0, halo_in[0])
+    halo_in[1] = jnp.where(me == STRIPS - 1, 0.0, halo_in[1])
+    top = lax.broadcasted_iota(jnp.int32, (8, 128), 0) == 0
+    bottom = lax.broadcasted_iota(jnp.int32, (8, 128), 0) == 7
+    far = lax.rem(lag + 2, LAGS)
+
+    def turn(blocks):
+        at = [lax.rem(2 * far + XB - 1 + n, XB) for n in blocks]
+
+        def one(p, carry):
+            for b in at:
+                parts = []
+                for n in range(2):
+                    k = 2 * p + n
+                    j = k * XB + b
+                    above = jnp.broadcast_to(halo_in[0, b, pl.ds(k, 1), :], (8, 128))
+                    below = jnp.broadcast_to(halo_in[1, b, pl.ds(k, 1), :], (8, 128))
+                    first, last = smooth[j, 0:8, :], smooth[j, ROWS - 8 : ROWS, :]
+                    parts += [
+                        jnp.where(top, first - above, first),
+                        smooth[j, 8 : ROWS - 8, :],
+                        jnp.where(bottom, last - below, last),
+                    ]
+                x = 128 * b
+                sides = columns[p, pl.ds(x + 7, 128), :] + columns[p, pl.ds(x + 9, 128), :]
+                base = pl.multiple_of(PADF + p * NX + x, 8)
+                filt[pl.ds(base, 128), :] = jnp.concatenate(parts, axis=0).T - sides
+            return carry
+
+        lax.fori_loop(0, PAIRS, one, 0, unroll=4)
+
+    turn(range(0, 4))
 
     first_lag = lag * NK - NK * LAGS // 2
 
@@ -259,7 +271,6 @@
                 half, pltpu.roll(c, ROWS, 1), d
             )
 
-        far = lax.rem(lag + 2, LAGS)
         products(far, 0, part.at[q, 0, 0])
         far_up = lag_copy(6 * q, part.at[q, 0, 0], relay.at[q, 0], up_lag)
         far_up.start()
@@ -299,7 +310,7 @@
     copies = []
     for q in range(4):
         copies.append(
-            adjoint(q, (lambda q=q: pass_on(q - 1, copies[q - 1])) if q else lambda: None)
+            adjoint(q, (lambda q=q: pass_on(q - 1, copies[q - 1])) if q else lambda: turn(range(4, 8)))
         )
     pass_on(3, copies[3])
     for q in range(4):

time: 47.2 us -> 47.9 us (1.015)
  Pallas kernels: 46.5 us -> 47 us
    pallas_call x1, Pallas kernels: 45.5 us -> 46.1 us  [local(): pl.pallas_call(kernel, out_shape=jax.ShapeDtypeStruct((4, OUTX // SUB, HA...]
where the time goes in v8:
time: 47.9 us; the launch traced here: 47.7 us
  Pallas kernels  47 us (98%)
  between operations  0.64 us (1%)
    pallas_call x1, Pallas kernels, local(): pl.pallas_call(kernel, out_shape=jax.ShapeDtypeStruct((4, OUTX // SUB, HA...  46.1 us
    pallas_call x1, Pallas kernels, local(): pl.pallas_call(turned, out_shape=(out, out), in_specs=[pl.BlockSpec(memor...  0.97 us

profile of v8, /device:TPU:1, one launch (start us, length us, event | category | flops | bytes accessed | tf_op | source)
XLA Modules:
  0.0 47.7 jit_solution(6896128962802913104)
XLA Ops:
  0.6 46.1 %adjoint.1.result = f32[4,2,64,128]{3,2,1,0:T(8,128)S(1)} custom-call(f32[32,64,1024]{2,1,0:T(8,128)} %grad.1, f32[2,16,4096]{2,1,0:T(8,128)} %bitcast.2, f32[2,16,4096]{2,1,0:T(8,128)} %bitcast.3), custom_call_target="tpu_custom_call" | custom-call | tf_op jit(solution)/shard_map/adjoint/pallas_call | solution.py:337
  46.7 1.0 %turned.1 = (f32[2,64,256]{2,1,0:T(8,128)}, f32[2,64,256]{2,1,0:T(8,128)}) custom-call(f32[4,2,64,128]{3,2,1,0:T(8,128)S(1)} %adjoint.1.result), custom_call_target="tpu_custom_call" | custom-call | tf_op jit(solution)/shard_map/turned/pallas_call | solution.py:376

commit v9 on v6

--- a/solution.py
+++ b/solution.py
@@ -152,7 +152,8 @@
         rows = pl.ds(n * (PADD + NX), PADD)
         twice[rows, :] = jnp.zeros((PADD, 128), F32)
         rows = pl.ds(n * (PADX + NX), PADX)
-        field[rows, :] = jnp.zeros((PADX, 128), F32)
+        for m in range(2):
+            field[m, rows, :] = jnp.zeros((PADX, 128), F32)
         rows = pl.ds(n * (PADF + PAIRS * NX), PADF)
         filt[rows, :] = jnp.zeros((PADF, 128), F32)
 
@@ -215,8 +216,11 @@
 
     low_x = lax.broadcasted_iota(jnp.int32, (EXP, 128), 1) < ROWS
 
-    def adjoint(q, between):
-        sign = 1 if PHASES[q][0] == 1 else -1
+    def sign_of(q):
+        return 1 if PHASES[q][0] == 1 else -1
+
+    def arrive(q):
+        sign = sign_of(q)
         land[q, here, :] = packed[q, me]
         if q < len(SENDS):
             copy_bytes(packed.at[SENDS[q], 0 : STRIPS - 1], a2a_recv.at[q]).wait()
@@ -234,55 +238,65 @@
         def expand(i, carry):
             at = pl.multiple_of(PADD - 8 + i * EXP, 8)
             to = pl.ds(pl.multiple_of(PADX - 8 + i * EXP, 8), EXP)
-            field[to, :] = jnp.where(low_x, twice[pl.ds(at, EXP), :], twice[pl.ds(at + sign, EXP), :])
+            field[q % 2, to, :] = jnp.where(low_x, twice[pl.ds(at, EXP), :], twice[pl.ds(at + sign, EXP), :])
             return carry
 
         lax.fori_loop(0, (NX + 16) // EXP, expand, 0)
 
-        half = lax.broadcasted_iota(jnp.int32, (HALF, 128), 1) < ROWS
-        start = 0 if sign == 1 else -8
-
-        def products(block, i, out):
-            x = block * OUTX + i * SUB + start
-
-            def step(p, total):
-                h = (first_lag + 2 * p) * sign
-                g = filt[pl.ds(PADF + p * NX + x + h, SUBX), :]
-                return total + g * field[pl.ds(PADX + x + 2 * h, SUBX), :]
-
-            sums[...] = lax.fori_loop(0, PAIRS, step, jnp.zeros((SUBX, 128), F32), unroll=4)
-            at = 0 if sign == 1 else 8
-            a, b = sums[at : at + HALF], sums[at + HALF : at + SUB]
-            at += sign
-            c, d = sums[at : at + HALF], sums[at + HALF : at + SUB]
-            out[...] = jnp.where(half, a, pltpu.roll(b, ROWS, 1)) + jnp.where(
-                half, pltpu.roll(c, ROWS, 1), d
-            )
-
-        far = lax.rem(lag + 2, LAGS)
-        products(far, 0, part.at[q, 0, 0])
+    half = lax.broadcasted_iota(jnp.int32, (HALF, 128), 1) < ROWS
+
+    def products(q, block, i, out):
+        sign = sign_of(q)
+        x = block * OUTX + i * SUB + (0 if sign == 1 else -8)
+
+        def step(p, total):
+            h = (first_lag + 2 * p) * sign
+            g = filt[pl.ds(PADF + p * NX + x + h, SUBX), :]
+            return total + g * field[q % 2, pl.ds(PADX + x + 2 * h, SUBX), :]
+
+        sums[...] = lax.fori_loop(0, PAIRS, step, jnp.zeros((SUBX, 128), F32), unroll=4)
+        at = 0 if sign == 1 else 8
+        a, b = sums[at : at + HALF], sums[at + HALF : at + SUB]
+        at += sign
+        c, d = sums[at : at + HALF], sums[at + HALF : at + SUB]
+        out[...] = jnp.where(half, a, pltpu.roll(b, ROWS, 1)) + jnp.where(
+            half, pltpu.roll(c, ROWS, 1), d
+        )
+
+    far_lag = lax.rem(lag + 2, LAGS)
+
+    def copies_of(q):
         far_up = lag_copy(6 * q, part.at[q, 0, 0], relay.at[q, 0], up_lag)
-        far_up.start()
-        products(far, 1, part.at[q, 0, 1])
         far_down = lag_copy(6 * q + 1, part.at[q, 0, 1], relay.at[q, 1], down_lag)
-        far_down.start()
-        between()
-        products(up_lag, 1, part.at[q, 1, 1])
         up_1 = lag_copy(6 * q + 2, part.at[q, 1, 1], near_in.at[q, 0, 1], up_lag)
-        up_1.start()
-        products(down_lag, 0, part.at[q, 2, 0])
         down_0 = lag_copy(6 * q + 3, part.at[q, 2, 0], near_in.at[q, 1, 0], down_lag)
-        down_0.start()
-        products(up_lag, 0, part.at[q, 1, 0])
-        products(down_lag, 1, part.at[q, 2, 1])
-        products(lag, 0, own.at[q, 0])
-        products(lag, 1, own.at[q, 1])
         up_0 = lag_copy(6 * q + 4, part.at[q, 1, 0], near_in.at[q, 0, 0], up_lag)
         down_1 = lag_copy(6 * q + 5, part.at[q, 2, 1], near_in.at[q, 1, 1], down_lag)
         return far_up, far_down, up_1, down_0, up_0, down_1
 
-    def pass_on(q, copies):
-        far_up, far_down, _, _, up_0, down_1 = copies
+    copies = [copies_of(q) for q in range(4)]
+
+    def far(q):
+        arrive(q)
+        products(q, far_lag, 0, part.at[q, 0, 0])
+        copies[q][0].start()
+        products(q, far_lag, 1, part.at[q, 0, 1])
+        copies[q][1].start()
+
+    def direct(q):
+        products(q, up_lag, 1, part.at[q, 1, 1])
+        copies[q][2].start()
+        products(q, down_lag, 0, part.at[q, 2, 0])
+        copies[q][3].start()
+
+    def joined(q):
+        products(q, up_lag, 0, part.at[q, 1, 0])
+        products(q, down_lag, 1, part.at[q, 2, 1])
+        products(q, lag, 0, own.at[q, 0])
+        products(q, lag, 1, own.at[q, 1])
+
+    def pass_on(q):
+        far_up, far_down, _, _, up_0, down_1 = copies[q]
         far_up.wait_recv()
         part[q, 1, 0] = part[q, 1, 0] + relay[q, 0]
         up_0.start()
@@ -290,20 +304,26 @@
         part[q, 2, 1] = part[q, 2, 1] + relay[q, 1]
         down_1.start()
 
-    def finish(q, copies):
-        far_up, far_down, up_1, down_0, up_0, down_1 = copies
-        for copy in (up_1, down_0, up_0, down_1):
+    def finish(q):
+        for copy in copies[q][2:]:
             copy.wait_recv()
         result[q] = 0.25 * (own[q] + near_in[q, 0] + near_in[q, 1])
 
-    copies = []
+    for first in (0, 2):
+        pair = (first, first + 1)
+        for q in pair:
+            far(q)
+        if first:
+            pass_on(0)
+            pass_on(1)
+        for q in pair:
+            direct(q)
+        for q in pair:
+            joined(q)
+    pass_on(2)
+    pass_on(3)
     for q in range(4):
-        copies.append(
-            adjoint(q, (lambda q=q: pass_on(q - 1, copies[q - 1])) if q else lambda: None)
-        )
-    pass_on(3, copies[3])
-    for q in range(4):
-        finish(q, copies[q])
+        finish(q)
 
     for q in range(4):
         for copy in copies[q]:
@@ -338,7 +358,7 @@
             vmem((4, COLS, STRIPS * ROWS), F32),
             vmem((4, STRIPS * PIECE, 128), F32),
             vmem((NX + 2 * PADD, 128), F32),
-            vmem((NX + 2 * PADX, 128), F32),
+            vmem((2, NX + 2 * PADX, 128), F32),
             vmem((2, XB, NK, 128), F32),
             vmem((2, XB, NK, 128), F32),
             vmem((SUBX, 128), F32),

time: 47.2 us -> 45.5 us (0.964); the launches traced: 47.1 us -> 44.8 us
  Pallas kernels: 46.5 us -> 44.1 us
    pallas_call x1, Pallas kernels: 45.5 us -> 43.2 us  [local(): pl.pallas_call(kernel, out_shape=jax.ShapeDtypeStruct((4, OUTX // SUB, HA...]
where the time goes in v9:
time: 45.5 us; the launch traced here: 44.8 us
  Pallas kernels  44.1 us (97%)
  between operations  0.64 us (1%)
    pallas_call x1, Pallas kernels, local(): pl.pallas_call(kernel, out_shape=jax.ShapeDtypeStruct((4, OUTX // SUB, HA...  43.2 us
    pallas_call x1, Pallas kernels, local(): pl.pallas_call(turned, out_shape=(out, out), in_specs=[pl.BlockSpec(memor...  0.97 us

profile of v9, /device:TPU:1, one launch (start us, length us, event | category | flops | bytes accessed | tf_op | source)
XLA Modules:
  0.0 44.8 jit_solution(4260798977110467651)
XLA Ops:
  0.6 43.2 %adjoint.1.result = f32[4,2,64,128]{3,2,1,0:T(8,128)S(1)} custom-call(f32[32,64,1024]{2,1,0:T(8,128)} %grad.1, f32[2,16,4096]{2,1,0:T(8,128)} %bitcast.2, f32[2,16,4096]{2,1,0:T(8,128)} %bitcast.3), custom_call_target="tpu_custom_call" | custom-call | tf_op jit(solution)/shard_map/adjoint/pallas_call | solution.py:346
  43.8 1.0 %turned.1 = (f32[2,64,256]{2,1,0:T(8,128)}, f32[2,64,256]{2,1,0:T(8,128)}) custom-call(f32[4,2,64,128]{3,2,1,0:T(8,128)S(1)} %adjoint.1.result), custom_call_target="tpu_custom_call" | custom-call | tf_op jit(solution)/shard_map/turned/pallas_call | solution.py:385

commit v10 on v9

--- a/solution.py
+++ b/solution.py
@@ -114,6 +114,18 @@
         copy_bytes(raw.at[q], raw_sem.at[q]).wait()
         lax.fori_loop(0, STRIPS // 2, one, 0, unroll=8)
 
+    tile_rows = tiles.reshape(NK * XB * SLOT, 128)
+    for row in (7, 8 + ROWS):
+        tile_rows[pl.ds(row, NK * XB, stride=SLOT), :] = jnp.zeros((NK * XB, 128), F32)
+    for n in range(2):
+        rows = pl.ds(n * (PADD + NX), PADD)
+        twice[rows, :] = jnp.zeros((PADD, 128), F32)
+        rows = pl.ds(n * (PADX + NX), PADX)
+        for m in range(2):
+            field[m, rows, :] = jnp.zeros((PADX, 128), F32)
+        rows = pl.ds(n * (PADF + PAIRS * NX), PADF)
+        filt[rows, :] = jnp.zeros((PADF, 128), F32)
+
     pack(0)
 
     copy_bytes(edge, edge_sem).wait()
@@ -147,20 +159,6 @@
     send_field(SENDS[0])
     pack(1)
     send_field(SENDS[1])
-
-    for n in range(2):
-        rows = pl.ds(n * (PADD + NX), PADD)
-        twice[rows, :] = jnp.zeros((PADD, 128), F32)
-        rows = pl.ds(n * (PADX + NX), PADX)
-        for m in range(2):
-            field[m, rows, :] = jnp.zeros((PADX, 128), F32)
-        rows = pl.ds(n * (PADF + PAIRS * NX), PADF)
-        filt[rows, :] = jnp.zeros((PADF, 128), F32)
-
-    tile_rows = tiles.reshape(NK * XB * SLOT, 128)
-    blank = jnp.zeros((NK * XB, 128), F32)
-    for row in (7, 8 + ROWS):
-        tile_rows[pl.ds(row, NK * XB, stride=SLOT), :] = blank
 
     def prepare(p, carry):
         columns[p, 0:8, :] = jnp.zeros((8, 128), F32)
@@ -188,24 +186,38 @@
 
     halo_up.wait()
     halo_down.wait()
-    smooth_rows = smooth.reshape(NK * XB * ROWS, 128)
-    for b in range(XB):
-        first = pl.ds(ROWS * b, NK, stride=ROWS * XB)
-        last = pl.ds(ROWS * b + ROWS - 1, NK, stride=ROWS * XB)
-        above = jnp.where(me == 0, 0.0, halo_in[0, b])
-        below = jnp.where(me == STRIPS - 1, 0.0, halo_in[1, b])
-        smooth_rows[first, :] = smooth_rows[first, :] - above
-        smooth_rows[last, :] = smooth_rows[last, :] - below
-
-    def turn(p, carry):
-        for b in range(XB):
-            both = [smooth[(2 * p + n) * XB + b] for n in range(2)]
-            sides = columns[p, 7 + 128 * b : 135 + 128 * b, :] + columns[p, 9 + 128 * b : 137 + 128 * b, :]
-            base = pl.multiple_of(PADF + p * NX + 128 * b, 8)
-            filt[pl.ds(base, 128), :] = jnp.concatenate(both, axis=0).T - sides
-        return carry
-
-    lax.fori_loop(0, PAIRS, turn, 0, unroll=2)
+    halo_in[0] = jnp.where(me == 0, 0.0, halo_in[0])
+    halo_in[1] = jnp.where(me == STRIPS - 1, 0.0, halo_in[1])
+    top = lax.broadcasted_iota(jnp.int32, (8, 128), 0) == 0
+    bottom = lax.broadcasted_iota(jnp.int32, (8, 128), 0) == 7
+    far_lag = lax.rem(lag + 2, LAGS)
+
+    def turn(blocks):
+        at = [lax.rem(2 * far_lag + XB - 1 + n, XB) for n in blocks]
+
+        def one(p, carry):
+            for b in at:
+                parts = []
+                for n in range(2):
+                    k = 2 * p + n
+                    j = k * XB + b
+                    above = jnp.broadcast_to(halo_in[0, b, pl.ds(k, 1), :], (8, 128))
+                    below = jnp.broadcast_to(halo_in[1, b, pl.ds(k, 1), :], (8, 128))
+                    first, last = smooth[j, 0:8, :], smooth[j, ROWS - 8 : ROWS, :]
+                    parts += [
+                        jnp.where(top, first - above, first),
+                        smooth[j, 8 : ROWS - 8, :],
+                        jnp.where(bottom, last - below, last),
+                    ]
+                x = 128 * b
+                sides = columns[p, pl.ds(x + 7, 128), :] + columns[p, pl.ds(x + 9, 128), :]
+                base = pl.multiple_of(PADF + p * NX + x, 8)
+                filt[pl.ds(base, 128), :] = jnp.concatenate(parts, axis=0).T - sides
+            return carry
+
+        lax.fori_loop(0, PAIRS, one, 0, unroll=2)
+
+    turn(range(XB))
 
     first_lag = lag * NK - NK * LAGS // 2
 
@@ -262,8 +274,6 @@
         out[...] = jnp.where(half, a, pltpu.roll(b, ROWS, 1)) + jnp.where(
             half, pltpu.roll(c, ROWS, 1), d
         )
-
-    far_lag = lax.rem(lag + 2, LAGS)
 
     def copies_of(q):
         far_up = lag_copy(6 * q, part.at[q, 0, 0], relay.at[q, 0], up_lag)

time: 45.5 us -> 45.5 us (level)
  no operation moved by 1% of the time
where the time goes in v10:
time: 45.5 us; the launch traced here: 44.7 us
  Pallas kernels  44.1 us (97%)
  between operations  0.64 us (1%)
    pallas_call x1, Pallas kernels, local(): pl.pallas_call(kernel, out_shape=jax.ShapeDtypeStruct((4, OUTX // SUB, HA...  43.1 us
    pallas_call x1, Pallas kernels, local(): pl.pallas_call(turned, out_shape=(out, out), in_specs=[pl.BlockSpec(memor...  0.97 us

profile of v10, /device:TPU:1, one launch (start us, length us, event | category | flops | bytes accessed | tf_op | source)
XLA Modules:
  0.0 44.7 jit_solution(10865971770867910016)
XLA Ops:
  0.6 43.1 %adjoint.1.result = f32[4,2,64,128]{3,2,1,0:T(8,128)S(1)} custom-call(f32[32,64,1024]{2,1,0:T(8,128)} %grad.1, f32[2,16,4096]{2,1,0:T(8,128)} %bitcast.2, f32[2,16,4096]{2,1,0:T(8,128)} %bitcast.3), custom_call_target="tpu_custom_call" | custom-call | tf_op jit(solution)/shard_map/adjoint/pallas_call | solution.py:356
  43.7 1.0 %turned.1 = (f32[2,64,256]{2,1,0:T(8,128)}, f32[2,64,256]{2,1,0:T(8,128)}) custom-call(f32[4,2,64,128]{3,2,1,0:T(8,128)S(1)} %adjoint.1.result), custom_call_target="tpu_custom_call" | custom-call | tf_op jit(solution)/shard_map/turned/pallas_call | solution.py:395
